TPU v7x, 32 devices: a whole 2x2x4 slice. The times are simulated.
32 devices in a mesh: group: 2 (over y), gene: 4 (over z), lat: 2 (over x), sub: 2 (over core).
Axes of the slice: x: 2, y: 2, z: 4, core: 2. Of those that a mesh axis runs over, the one named last changes fastest.
Arguments:
- cell_index: int32 [2048], P(('group', 'lat', 'sub')), parts along dimension 0, may hold values from 0 to 511
- coords_table: float32 [4, 2048], P('group', ('lat', 'sub')), parts along dimension 0, may hold values from 0 to 1
- expr_table: bfloat16 [4096, 16384], P(('group', 'lat', 'sub'), 'gene'), parts along dimension 0, may hold values from -6 to 6
- inducing: float32 [4, 64, 8192], P('group', 'lat', 'sub'), parts along dimension 0, may hold values from 0 to 1
- ind_weights: float32 [128, 8192], P(('group', 'lat'), 'sub'), parts along dimension 0, may hold values from -0.6 to 0.6
- lengthscale: float32 [128], P(('group', 'lat')), parts along dimension 0, may hold values from 0.02 to 0.1
- variance: float32 [128], P(('group', 'lat')), parts along dimension 0, may hold values from 0.5 to 2
- mixing: bfloat16 [128, 16384], P('group', 'gene'), parts along dimension 0, may hold values from -0.75 to 0.75
- noise_prec: float32 [32768], P(('group', 'gene')), parts along dimension 0, may hold values from 0.5 to 4
Outputs:
- grad_mixing: float32 [128, 16384], P('group', 'gene'), parts along dimension 0
- grad_inducing: float32 [128, 8192], P(('group', 'lat'), 'sub'), parts along dimension 0
There are 2 independent parts, one for each index of `group`. A program takes and returns all parts, laid end to end along the dimension named above; each array names one. Nothing has to cross between parts.
Inputs may be any that keep to these rules, and one draw needn't show every extreme that they name: Entry n indexes a row inside block n // 256 of the tables: cell n is table row (n // 256) * 512 + cell_index[n]; cells may repeat.
All inputs are finite; a program needn't handle non-finite values.
Results may differ from a plain program's by a relative error of at most 0.00075.
Values may be sent and summed in bfloat16 or wider, within the bound.
A program may use at most 64 MiB of HBM per device.

v0:
```python
import functools
import math

import jax
import jax.numpy as jnp
from jax import lax
from jax.experimental import pallas as pl
from jax.experimental.pallas import tpu as pltpu
from jax.sharding import PartitionSpec as P

F32 = jnp.float32
BF16 = jnp.bfloat16
GROUP = 8
DEPTH = 24
SPARE = 21
CENTER = 0.5


def pieces(value):
    high = value.astype(BF16).astype(F32)
    rest = value - high
    middle = rest.astype(BF16).astype(F32)
    low = (rest - middle).astype(BF16).astype(F32)
    return high, middle, low


def pieces_outside(value):
    high = lax.reduce_precision(value, 8, 7)
    rest = value - high
    middle = lax.reduce_precision(rest, 8, 7)
    low = lax.reduce_precision(rest - middle, 8, 7)
    return high, middle, low


LEFT = (0, 0, 1, 1, 0, 2)
RIGHT = (0, 1, 0, 1, 2, 0)


def cell_features(xy):
    x, y = xy[0] - CENTER, xy[1] - CENTER
    px, py, pn = pieces_outside(x), pieces_outside(y), pieces_outside(x * x + y * y)
    one, zero = jnp.ones_like(x), jnp.zeros_like(x)
    columns = [px[i] for i in LEFT] + [py[i] for i in LEFT] + [pn[i] for i in LEFT]
    columns += [one] * 3 + [zero] * (DEPTH - SPARE)
    return jnp.stack(columns, axis=1).astype(BF16)


def point_features(points_ref, length_ref, extra, table_ref):
    length = length_ref[...]
    scale = 0.5 / (length * length)
    x = points_ref[0] - CENTER
    y = points_ref[1] - CENTER
    px = pieces(x * (2.0 * scale))
    py = pieces(y * (2.0 * scale))
    ps = pieces(jnp.broadcast_to(-scale, x.shape))
    pn = pieces((x * x + y * y) * -scale)
    rows = [px[i] for i in RIGHT] + [py[i] for i in RIGHT] + [ps[i] for i in RIGHT]
    rows += list(pn) + [extra] + [jnp.zeros_like(x)] * (DEPTH - SPARE - 1)
    for place, row in enumerate(rows):
        for lane in range(GROUP):
            table_ref[lane, place : place + 1, :] = row[lane : lane + 1, :]


def forward_body(tile, feat_ref, points_ref, weight_ref, length_ref, height_ref, out_ref, table_ref, wide_ref):
    point_features(points_ref, length_ref, weight_ref[...], table_ref)
    feat = feat_ref[...]
    count = weight_ref.shape[1]

    def one(j, carry):
        total = jnp.zeros((feat.shape[0], 128), F32)
        for start in range(0, count, tile):
            part = table_ref[j, :, start : start + tile].astype(BF16)
            value = jnp.exp(jnp.dot(feat, part, preferred_element_type=F32))
            for lane in range(0, tile, 128):
                w = table_ref[j, SPARE : SPARE + 1, start + lane : start + lane + 128]
                total = total + value[:, lane : lane + 128] * w
        wide_ref[j] = total
        return carry

    lax.fori_loop(0, GROUP, one, 0)
    for j in range(GROUP):
        total = jnp.sum(wide_ref[j].T, axis=0, keepdims=True)
        total = total * height_ref[j : j + 1, :]
        blocks, _, width = out_ref.shape
        for block in range(blocks):
            out_ref[block, j : j + 1, :] = total[:, block * width : (block + 1) * width]


def backward_body(
    tile, feat_ref, points_ref, grad_ref, length_ref, height_ref, out_ref, table_ref, wide_ref, sum_ref
):
    count = points_ref.shape[2]
    point_features(points_ref, length_ref, jnp.zeros((GROUP, count), F32), table_ref)
    feat = feat_ref[...]
    rows = feat.shape[0]
    grad = (grad_ref[...] * height_ref[...]).T
    for j in range(GROUP):
        wide_ref[j] = jnp.broadcast_to(grad[:, j : j + 1], (rows, 128))

    def one(j, carry):
        for start in range(0, count, tile):
            part = table_ref[j, :, start : start + tile].astype(BF16)
            value = jnp.exp(jnp.dot(feat, part, preferred_element_type=F32))
            for lane in range(0, tile, 128):
                term = value[:, lane : lane + 128] * wide_ref[j]
                sum_ref[j, :, start + lane : start + lane + 128] = jnp.sum(
                    term.reshape(rows // 8, 8, 128), axis=0
                )
        return carry

    lax.fori_loop(0, GROUP, one, 0)
    for j in range(GROUP):
        out_ref[j : j + 1, :] = jnp.sum(sum_ref[j], axis=0, keepdims=True)


def middle_body(scale, index_ref, expr_ref, latent_ref, mixing_ref, noise_ref, mix_out_ref, chunk_ref, cell_ref):
    rows = index_ref.shape[0]
    table = expr_ref.shape[0]
    pick = (lax.broadcasted_iota(jnp.int32, (rows, table), 1) == index_ref[...]).astype(F32).astype(BF16)
    observed = jnp.dot(pick, expr_ref[...], preferred_element_type=F32)
    latent = latent_ref[...]
    mixing = mixing_ref[...]
    predicted = lax.dot_general(latent, mixing, (((0,), (0,)), ((), ())), preferred_element_type=F32)
    weighted = (noise_ref[...] * (observed - predicted)).astype(BF16)
    mix_out_ref[...] = scale * jnp.dot(latent, weighted, preferred_element_type=F32)

    @pl.when(pl.program_id(0) == 0)
    def _():
        cell_ref[...] = jnp.zeros_like(cell_ref)

    cell_ref[...] += scale * lax.dot_general(
        mixing, weighted, (((1,), (1,)), ((), ())), preferred_element_type=F32
    )

    @pl.when(pl.program_id(0) == pl.num_programs(0) - 1)
    def _():
        genes, lats, depth, width = chunk_ref.shape
        for gene in range(genes):
            for lat in range(lats):
                chunk_ref[gene, lat] = cell_ref[
                    lat * depth : (lat + 1) * depth, gene * width : (gene + 1) * width
                ]


AXES = ("gene", "lat", "sub")


def place_of(rank, sizes):
    return rank // (sizes[1] * sizes[2]), rank // sizes[2] % sizes[1], rank % sizes[2]


def greet(ranks):
    barrier = pltpu.get_barrier_semaphore()
    for device in ranks:
        pl.semaphore_signal(barrier, inc=1, device_id=device, device_id_type=pl.DeviceIdType.MESH)
    pl.semaphore_wait(barrier, len(ranks))


def exchange_body(sizes, chunk_of, finish, send_ref, out_ref, recv_ref, send_sem, recv_sem, own_sem):
    total = sizes[0] * sizes[1] * sizes[2]
    place = tuple(lax.axis_index(axis) for axis in AXES)
    me = (place[0] * sizes[1] + place[1]) * sizes[2] + place[2]
    peers = [place_of(lax.rem(me + k, total), sizes) for k in range(1, total)]
    greet([dict(zip(AXES, peer)) for peer in peers])
    copies = []
    for k, peer in enumerate(peers):
        copy = pltpu.make_async_remote_copy(
            src_ref=send_ref.at[chunk_of(peer)],
            dst_ref=recv_ref.at[me],
            send_sem=send_sem.at[k],
            recv_sem=recv_sem.at[k],
            device_id=dict(zip(AXES, peer)),
            device_id_type=pl.DeviceIdType.MESH,
        )
        copy.start()
        copies.append(copy)
    own = pltpu.make_async_copy(send_ref.at[chunk_of(place)], recv_ref.at[me], own_sem)
    own.start()
    own.wait()
    for copy in copies:
        copy.wait()
    finish(recv_ref, out_ref)


def exchange(sizes, chunk_of, finish, out, collective_id, send):
    total = sizes[0] * sizes[1] * sizes[2]
    return pl.pallas_call(
        functools.partial(exchange_body, sizes, chunk_of, finish),
        in_specs=[pl.BlockSpec(memory_space=pltpu.VMEM)],
        out_specs=pl.BlockSpec(memory_space=pltpu.VMEM),
        out_shape=out,
        scratch_shapes=[
            pltpu.VMEM((total, *send.shape[1:]), F32),
            pltpu.SemaphoreType.DMA((total - 1,)),
            pltpu.SemaphoreType.DMA((total - 1,)),
            pltpu.SemaphoreType.DMA,
        ],
        compiler_params=pltpu.CompilerParams(collective_id=collective_id, has_side_effects=True),
    )(send)


def gene_sum_body(genes, x_ref, out_ref, recv_ref, sum_ref, all_ref, send_sem, recv_sem, back_sem, full_sem):
    me = lax.axis_index("gene")
    width = sum_ref.shape[1]
    peers = [lax.rem(me + k, genes) for k in range(1, genes)]
    greet([{"gene": peer} for peer in peers])

    def columns(place):
        return pl.ds(pl.multiple_of(place * width, 128), width)

    copies = []
    for k, peer in enumerate(peers):
        copy = pltpu.make_async_remote_copy(
            src_ref=x_ref.at[:, columns(peer)],
            dst_ref=recv_ref.at[k],
            send_sem=send_sem.at[k],
            recv_sem=recv_sem.at[k],
            device_id={"gene": peer},
            device_id_type=pl.DeviceIdType.MESH,
        )
        copy.start()
        copies.append(copy)
    for copy in copies:
        copy.wait()
    value = x_ref[:, columns(me)]
    for k in range(genes - 1):
        value = value + recv_ref[k]
    sum_ref[...] = value
    backs = []
    for k, peer in enumerate(peers):
        copy = pltpu.make_async_remote_copy(
            src_ref=sum_ref,
            dst_ref=all_ref.at[k],
            send_sem=back_sem.at[k],
            recv_sem=full_sem.at[k],
            device_id={"gene": peer},
            device_id_type=pl.DeviceIdType.MESH,
        )
        copy.start()
        backs.append(copy)
    out_ref[:, columns(me)] = value
    for k, copy in enumerate(backs):
        copy.wait()
        out_ref[:, columns(lax.rem(me + genes - 1 - k, genes))] = all_ref[k]


def gene_sum(genes, collective_id, x):
    rows, count = x.shape
    width = count // genes
    sems = pltpu.SemaphoreType.DMA((genes - 1,))
    return pl.pallas_call(
        functools.partial(gene_sum_body, genes),
        in_specs=[pl.BlockSpec(memory_space=pltpu.VMEM)],
        out_specs=pl.BlockSpec(memory_space=pltpu.VMEM),
        out_shape=jax.ShapeDtypeStruct(x.shape, F32),
        scratch_shapes=[
            pltpu.VMEM((genes - 1, rows, width), F32),
            pltpu.VMEM((rows, width), F32),
            pltpu.VMEM((genes - 1, rows, width), F32),
            sems,
            sems,
            sems,
            sems,
        ],
        compiler_params=pltpu.CompilerParams(
            collective_id=collective_id, has_side_effects=True, vmem_limit_bytes=40 * 2**20
        ),
    )(x)


def products(body, out_shape, scratch, feat, points, other, length, height):
    lats, count = points.shape[1], points.shape[2]
    rows = feat.shape[0]
    tile = min(256, count)
    work = rows * lats * count
    return pl.pallas_call(
        functools.partial(body, tile),
        grid=(lats // GROUP,),
        in_specs=[
            pl.BlockSpec((rows, DEPTH), lambda i: (0, 0)),
            pl.BlockSpec((2, GROUP, count), lambda i: (0, i, 0)),
            pl.BlockSpec((GROUP, other.shape[1]), lambda i: (i, 0)),
            pl.BlockSpec((GROUP, 1), lambda i: (i, 0)),
            pl.BlockSpec((GROUP, 1), lambda i: (i, 0)),
        ],
        out_specs=pl.BlockSpec(
            (*out_shape[:-2], GROUP, out_shape[-1]), lambda i: (*(0 for _ in out_shape[2:]), i, 0)
        ),
        out_shape=jax.ShapeDtypeStruct(out_shape, F32),
        scratch_shapes=[pltpu.VMEM((GROUP, DEPTH, count), F32), *scratch],
        cost_estimate=pl.CostEstimate(
            flops=2 * DEPTH * work, transcendentals=work, bytes_accessed=12 * lats * count
        ),
        compiler_params=pltpu.CompilerParams(vmem_limit_bytes=40 * 2**20),
    )(feat, points, other, length[:, None], height[:, None])


def middle(scale, chunks, cell_index, expr_table, latent, mixing, noise_prec):
    rows = cell_index.shape[0]
    table, genes = expr_table.shape
    lats = latent.shape[0]
    tile = min(512, genes)
    return pl.pallas_call(
        functools.partial(middle_body, scale),
        grid=(genes // tile,),
        in_specs=[
            pl.BlockSpec((rows, 1), lambda i: (0, 0)),
            pl.BlockSpec((table, tile), lambda i: (0, i)),
            pl.BlockSpec((lats, rows), lambda i: (0, 0)),
            pl.BlockSpec((lats, tile), lambda i: (0, i)),
            pl.BlockSpec((1, tile), lambda i: (0, i)),
        ],
        out_specs=[
            pl.BlockSpec((lats, tile), lambda i: (0, i)),
            pl.BlockSpec(chunks, lambda i: (0, 0, 0, 0)),
        ],
        out_shape=[
            jax.ShapeDtypeStruct((lats, genes), F32),
            jax.ShapeDtypeStruct(chunks, F32),
        ],
        scratch_shapes=[pltpu.VMEM((lats, rows), F32)],
        compiler_params=pltpu.CompilerParams(vmem_limit_bytes=40 * 2**20),
    )(cell_index[:, None], expr_table, latent, mixing, noise_prec[None, :])


def on_device(
    cell_index,
    coords_table,
    expr_table,
    inducing,
    ind_weights,
    lengthscale,
    variance,
    mixing,
    noise_prec,
):
    gene_count = lax.axis_size("gene")
    lat_count = lax.axis_size("lat")
    sub_count = lax.axis_size("sub")
    bat_rows = cell_index.shape[0]
    per_block = bat_rows // gene_count
    block_count = lat_count * sub_count
    gene_place = lax.axis_index("gene")
    mine = lax.dynamic_slice_in_dim(cell_index, gene_place * per_block, per_block, 0)
    picks = mine[:, None] == jnp.arange(coords_table.shape[1], dtype=mine.dtype)[None, :]
    local_xy = jnp.sum(jnp.where(picks[None], coords_table[:, None, :], 0.0), axis=2)
    kernel_xy = lax.all_gather(local_xy, ("lat", "sub"), axis=1, tiled=True)
    feat = cell_features(kernel_xy)
    rows = feat.shape[0]
    lats, count = ind_weights.shape
    local_latent = products(
        forward_body, (block_count, lats, per_block), [pltpu.VMEM((GROUP, rows, 128), F32)], feat, inducing, ind_weights, lengthscale, variance
    )
    sizes = (gene_count, lat_count, sub_count)

    def finish_latent(recv_ref, out_ref):
        for gene in range(gene_count):
            for lat in range(lat_count):
                first = (gene * lat_count + lat) * sub_count
                value = recv_ref[first]
                for sub in range(1, sub_count):
                    value = value + recv_ref[first + sub]
                out_ref[lat * lats : (lat + 1) * lats, gene * per_block : (gene + 1) * per_block] = value

    def finish_grad(recv_ref, out_ref):
        for block in range(block_count):
            value = recv_ref[block]
            for gene in range(1, gene_count):
                value = value + recv_ref[gene * block_count + block]
            out_ref[:, block * per_block : (block + 1) * per_block] = value

    latent = exchange(
        sizes,
        lambda peer: peer[1] * sub_count + peer[2],
        finish_latent,
        jax.ShapeDtypeStruct((lat_count * lats, bat_rows), F32),
        0,
        local_latent,
    ).astype(BF16)
    grad_scale = -1.0 / math.sqrt(bat_rows * block_count)
    chunks = (gene_count, lat_count, lats, per_block)
    mixing_term, cell_term = middle(grad_scale, chunks, cell_index, expr_table, latent, mixing, noise_prec)
    grad_mixing = lax.psum(mixing_term, ("lat", "sub"))
    latent_grad = exchange(
        sizes,
        lambda peer: peer[0] * lat_count + peer[1],
        finish_grad,
        jax.ShapeDtypeStruct((lats, rows), F32),
        1,
        cell_term.reshape(gene_count * lat_count, lats, per_block),
    )
    scratch = [pltpu.VMEM((GROUP, rows, 128), F32), pltpu.VMEM((GROUP, 8, count), F32)]
    partial_inducing = products(
        backward_body, (lats, count), scratch, feat, inducing, latent_grad, lengthscale, variance
    )
    grad_inducing = gene_sum(gene_count, 2, partial_inducing)
    return (grad_mixing, grad_inducing)


def solution(mesh):
    in_specs = (
        P(("group", "lat", "sub")),
        P("group", ("lat", "sub")),
        P(("group", "lat", "sub"), "gene"),
        P("group", "lat", "sub"),
        P(("group", "lat"), "sub"),
        P(("group", "lat")),
        P(("group", "lat")),
        P("group", "gene"),
        P(("group", "gene")),
    )
    out_specs = (P("group", "gene"), P(("group", "lat"), "sub"))
    return jax.shard_map(
        on_device, mesh=mesh, in_specs=in_specs, out_specs=out_specs, check_vma=False
    )
```

profile of v0, /device:TPU:0, one launch (start us, length us, event | category | flops | bytes accessed | tf_op | source)
XLA Modules:
  0.0 149.5 jit_solution(13949871368242998171)
XLA Ops:
  7.2 0.0 all-reduce.2.cloned.1.call-start
  7.2 0.7 copy.45.length_ref
  8.0 0.7 copy.46.height_ref
  8.7 0.8 dynamic_slice.3
  9.4 0.1 iota_compare_fusion
  9.5 0.8 select_reduce_fusion
  10.3 6.0 %all-gather = f32[4,64,2]{1,2,0:T(2,128)S(1)} all-gather(f32[1,64,2]{1,2,0:T(2,128)S(1)} %bitcast.36), channel_id=1, replica_groups=mesh['group'=2,'gene'=4,'lat'=2,'sub'=2] {'lat','sub'}, dimensions={0}, use_global_device_ids=true | all-gather | bytes 2560 | tf_op jit(solution)/shard_map/all_gather | solution.py:347
  16.3 0.1 reshape.146
  16.5 0.1 stack.9
  16.6 0.1 copy.44.feat_ref
  16.7 1.2 copy-done.6
  18.0 1.0 copy-done.8
  19.0 28.5 %shard_map.104.send_ref = f32[4,32,64]{2,1,0:T(8,128)S(1)} custom-call(bf16[256,24]{1,0:T(8,128)(2,1)S(1)} %copy.44.feat_ref, f32[2,32,4096]{2,1,0:T(8,128)S(1)} %copy-done.6, f32[32,4096]{1,0:T(8,128)S(1)} %copy-done.8, f32[32,1]{1,0:T(8,128)S(1)} %copy.45.length_ref, f32[32,1]{1,0:T(8,128)S(1)} %copy.46.height_ref), custom_call_target="tpu_custom_call" | custom-call | flops 1610612736 | bytes 1572864 | tf_op jit(solution)/shard_map/pallas_call | solution.py:276
  47.5 0.6 copy-done.3
  48.1 11.7 %shard_map.105 = f32[64,256]{1,0:T(8,128)} custom-call(f32[4,32,64]{2,1,0:T(8,128)} %copy-done.3), custom_call_target="tpu_custom_call" | custom-call | tf_op jit(solution)/shard_map/pallas_call | solution.py:187
  59.9 0.8 convert_element_type.4.latent_ref
  60.7 0.0 copy-done.9
  60.7 0.1 copy.47.index_ref
  60.8 0.0 copy-done.1
  60.9 0.0 copy-done.5
  60.9 0.0 copy-start
  60.9 2.2 %copy-done = bf16[512,4096]{1,0:T(8,128)(2,1)S(1)} copy-done((bf16[512,4096]{1,0:T(8,128)(2,1)S(1)}, bf16[512,4096]{1,0:T(8,128)(2,1)}, u32[]{:S(2)}) %copy-start) | copy-done | bytes 4194328
  63.1 8.3 %shard_map.106 = (f32[64,4096]{1,0:T(8,128)}, f32[4,2,32,64]{3,2,1,0:T(8,128)S(1)}) custom-call(s32[256,1]{1,0:T(8,128)S(1)} %copy.47.index_ref, bf16[512,4096]{1,0:T(8,128)(2,1)S(1)} %copy-done, bf16[64,256]{1,0:T(8,128)(2,1)S(1)} %convert_element_type.4.latent_ref, bf16[64,4096]{1,0:T(8,128)(2,1)S(1)} %copy-done.1, f32[1,4096]{1,0:T(1,128)S(1)} %bitcast.34), custom_call_target="tpu_custom_call" | custom-call | tf_op jit(solution)/shard_map/pallas_call | solution.py:303
  71.3 0.7 copy-done.2
  72.0 0.0 all-reduce.2.cloned.1.call-update
  72.0 12.1 %shard_map.107.grad_ref = f32[32,256]{1,0:T(8,128)} custom-call(f32[8,32,64]{2,1,0:T(8,128)} %bitcast.33), custom_call_target="tpu_custom_call" | custom-call | tf_op jit(solution)/shard_map/pallas_call | solution.py:187
  84.2 0.7 copy-done.4
  84.9 28.2 %shard_map.108.x_ref = f32[32,4096]{1,0:T(8,128)S(1)} custom-call(bf16[256,24]{1,0:T(8,128)(2,1)S(1)} %copy.44.feat_ref, f32[2,32,4096]{2,1,0:T(8,128)S(1)} %copy-done.7, f32[32,256]{1,0:T(8,128)S(1)} %copy-done.4, f32[32,1]{1,0:T(8,128)S(1)} %copy.45.length_ref, f32[32,1]{1,0:T(8,128)S(1)} %copy.46.height_ref), custom_call_target="tpu_custom_call" | custom-call | flops 1610612736 | bytes 1572864 | tf_op jit(solution)/shard_map/pallas_call | solution.py:276
  113.2 26.4 %shard_map.109 = f32[32,4096]{1,0:T(8,128)S(1)} custom-call(f32[32,4096]{1,0:T(8,128)S(1)} %shard_map.108.x_ref), custom_call_target="tpu_custom_call" | custom-call | tf_op jit(solution)/shard_map/pallas_call | solution.py:251
  139.6 0.0 all-reduce.2.cloned.1.call-done
  139.6 2.3 %copy.53 = f32[64,4096]{1,0:T(8,128)} copy(f32[64,4096]{1,0:T(8,128)} %all-reduce.2.cloned.1.call-done) | data formatting | bytes 2097152
  141.9 0.8 copy.54
  (17 shorter events, 0.1 us)
Async XLA Ops:
  7.2 132.4 %all-reduce.2.cloned.1.call-start = ((), (), s32[]{:S(2)}) async-start(), calls=%async_computation | async-start | bytes 2097152 | tf_op jit(solution)/shard_map/psum | solution.py:383
  16.7 1.2 copy-start.6
  18.0 1.0 copy-start.8
  19.0 41.7 %copy-start.9 = (s32[256]{0:T(256)S(1)}, s32[256]{0:T(256)}, u32[]{:S(2)}) copy-start(s32[256]{0:T(256)} %param.9) | copy-start | bytes 3076
  19.0 41.9 %copy-start.1 = (bf16[64,4096]{1,0:T(8,128)(2,1)S(1)}, bf16[64,4096]{1,0:T(8,128)(2,1)}, u32[]{:S(2)}) copy-start(bf16[64,4096]{1,0:T(8,128)(2,1)} %mixing_ref.1) | copy-start | bytes 1572868
  19.0 41.9 %copy-start.5 = (f32[4096]{0:T(1024)S(1)}, f32[4096]{0:T(1024)}, u32[]{:S(2)}) copy-start(f32[4096]{0:T(1024)} %param.17) | copy-start | bytes 49156
  19.0 65.2 %copy-start.7 = (f32[2,32,4096]{2,1,0:T(8,128)S(1)}, f32[2,32,4096]{2,1,0:T(8,128)}, u32[]{:S(2)}) copy-start(f32[2,32,4096]{2,1,0:T(8,128)} %points_ref.3) | copy-start | bytes 3145732
  47.5 0.6 copy-start.3
  60.9 2.2 %copy-start = (bf16[512,4096]{1,0:T(8,128)(2,1)S(1)}, bf16[512,4096]{1,0:T(8,128)(2,1)}, u32[]{:S(2)}) copy-start(bf16[512,4096]{1,0:T(8,128)(2,1)} %expr_ref.1) | copy-start | bytes 12582916
  71.3 0.7 copy-start.2
  84.2 0.8 copy-start.4
Sparse Core Ops, SparseCore 0:
  72.1 39.3 all-reduce.1
where the time goes:
time: 151 us; the launch traced here: 150 us
  Pallas kernels  115 us (76%)
  between operations  14.2 us (9%)
  local copies, waits for them, and re-layouts  12.2 us (8%)
  blocking collectives  6.01 us (4%)
  other arithmetic  1.75 us (1%)
    pallas_call x2, Pallas kernels, products(): pl.pallas_call(functools.partial(body, tile), grid=(lats // GROUP,), in_s...  56.7 us
    pallas_call x1, Pallas kernels, gene_sum(): pl.pallas_call(functools.partial(gene_sum_body, genes), in_specs=[pl.Bloc...  26.4 us
    pallas_call x2, Pallas kernels, exchange(): pl.pallas_call(functools.partial(exchange_body, sizes, chunk_of, finish),...  23.9 us
    unnamed x23, local copies, waits for them, and re-layouts  9.65 us
    pallas_call x1, Pallas kernels, middle(): pl.pallas_call(functools.partial(middle_body, scale), grid=(genes // tile...  8.28 us
    all_gather x1, blocking collectives, on_device(): kernel_xy = lax.all_gather(local_xy, ('lat', 'sub'), axis=1, tiled=True)  6.01 us
  transfers between devices with their start and end apart: 1, of which 0 were waited for; matrix products, arithmetic and copies ran while one was open for 0% of the time, Pallas kernels for 45%

commit v1 on v0

v1 whole, which is shorter than its diff:
```python
import functools
import math
from typing import NamedTuple

import jax
import jax.numpy as jnp
from jax import lax
from jax.experimental import pallas as pl
from jax.experimental.pallas import tpu as pltpu
from jax.sharding import PartitionSpec as P

F32 = jnp.float32
BF16 = jnp.bfloat16
DEPTH = 24
SPARE = 21
CENTER = 0.5
LOG2E = math.log2(math.e)
LEFT = (0, 0, 1, 1, 0, 2)
RIGHT = (0, 1, 0, 1, 2, 0)


class Plan(NamedTuple):
    gene: int
    lat: int
    sub: int
    rows: int
    table: int
    lats: int
    count: int
    genes: int
    share: int
    split: int
    sliced: bool
    scale: float

    @property
    def blocks(self):
        return self.lat * self.sub

    @property
    def points(self):
        return self.count // self.split

    @property
    def owners(self):
        return self.gene // self.split

    @property
    def total(self):
        return self.lat * self.lats

    @property
    def tile(self):
        return min(256, self.points)

    @property
    def wide(self):
        return min(512, self.genes)


def pieces(value):
    high = value.astype(BF16).astype(F32)
    rest = value - high
    middle = rest.astype(BF16).astype(F32)
    low = (rest - middle).astype(BF16).astype(F32)
    return high, middle, low


def point_features(plan, scale, points_ref, weight_ref, table_ref):
    step = min(512, plan.points)

    def part(i, carry):
        cols = pl.ds(pl.multiple_of(i * step, 128), step)
        x = points_ref[0, :, cols] - CENTER
        y = points_ref[1, :, cols] - CENTER
        px = pieces(x * (2.0 * scale))
        py = pieces(y * (2.0 * scale))
        ps = pieces(jnp.broadcast_to(-scale, x.shape))
        pn = pieces((x * x + y * y) * -scale)
        rows = [px[k] for k in RIGHT] + [py[k] for k in RIGHT] + [ps[k] for k in RIGHT]
        rows += list(pn) + [weight_ref[:, cols]] + [jnp.zeros_like(x)] * (DEPTH - SPARE - 1)
        for place, row in enumerate(rows):
            for lane in range(plan.share):
                table_ref[lane, place : place + 1, cols] = row[lane : lane + 1, :]
        return carry

    lax.fori_loop(0, plan.points // step, part, 0)


def cell_features(plan, xy_ref, side_ref, feat_ref):
    side_ref[...] = jnp.zeros_like(side_ref)
    side_ref[18:21, :] = jnp.ones((3, plan.rows), F32)
    for block in range(plan.blocks):
        x = xy_ref[block, 0:1, :] - CENTER
        y = xy_ref[block, 1:2, :] - CENTER
        px, py, pn = pieces(x), pieces(y), pieces(x * x + y * y)
        rows = [px[k] for k in LEFT] + [py[k] for k in LEFT] + [pn[k] for k in LEFT]
        for place, row in enumerate(rows):
            side_ref[place : place + 1, :] = row
        feat_ref[block * plan.rows : (block + 1) * plan.rows, :] = side_ref[...].T[:, :DEPTH].astype(BF16)


def body(
    plan,
    index_ref,
    coords_ref,
    length_ref,
    height_ref,
    expr_hbm,
    points_hbm,
    weight_hbm,
    mixing_hbm,
    noise_hbm,
    mix_out,
    ind_out,
    expr_ref,
    points_ref,
    weight_ref,
    mixing_ref,
    noise_ref,
    pick_ref,
    xy_ref,
    side_ref,
    feat_ref,
    table_ref,
    wide_ref,
    part_ref,
    near_ref,
    final_ref,
    latent_recv,
    latent_ref,
    side_lat_ref,
    seen_ref,
    cell_ref,
    chunk_ref,
    rs_ref,
    own_ref,
    lg_ref,
    lgpad_ref,
    mix_ref,
    mix_near,
    mix_far,
    mix_two,
    sum_ref,
    all_ref,
    load_sem,
    xy_sem,
    near_sem,
    latent_sem,
    rs_sem,
    lg_sem,
    mix_sem,
    all_sem,
):
    genes, lats, subs = plan.gene, plan.lat, plan.sub
    rows, share = plan.rows, plan.share
    g, l, s = lax.axis_index("gene"), lax.axis_index("lat"), lax.axis_index("sub")
    owner, slab = g // plan.split, lax.rem(g, plan.split)
    me = l * subs + s

    def at(dg=0, dl=0, ds=0):
        place = {}
        if genes > 1:
            place["gene"] = lax.rem(g + dg, genes)
        if lats > 1:
            place["lat"] = lax.rem(l + dl, lats)
        if subs > 1:
            place["sub"] = lax.rem(s + ds, subs)
        return place

    def send(src, dst, sems, k, device):
        copy = pltpu.make_async_remote_copy(
            src_ref=src,
            dst_ref=dst,
            send_sem=sems.at[(0, *k)],
            recv_sem=sems.at[(1, *k)],
            device_id=device,
            device_id_type=pl.DeviceIdType.MESH,
        )
        return copy

    if plan.sliced:
        points_src, weight_src = points_hbm, weight_hbm
    else:
        mine = pl.ds(pl.multiple_of(owner * share, 8), share)
        cut = pl.ds(pl.multiple_of(slab * plan.points, 128), plan.points)
        points_src, weight_src = points_hbm.at[:, mine, cut], weight_hbm.at[mine, cut]
    loads = [
        pltpu.make_async_copy(points_src, points_ref, load_sem.at[0]),
        pltpu.make_async_copy(weight_src, weight_ref, load_sem.at[1]),
        pltpu.make_async_copy(expr_hbm, expr_ref, load_sem.at[2]),
        pltpu.make_async_copy(mixing_hbm, mixing_ref, load_sem.at[3]),
        pltpu.make_async_copy(noise_hbm, noise_ref, load_sem.at[4]),
    ]
    for load in loads:
        load.start()

    far = [(dg, dl, 0) for dg in range(genes) for dl in range(lats) if dg or dl]
    flat = [(0, dl, ds) for dl in range(lats) for ds in range(subs) if dl or ds]
    peers = sorted(set(far) | set(flat))
    barrier = pltpu.get_barrier_semaphore()
    for peer in peers:
        pl.semaphore_signal(barrier, inc=1, device_id=at(*peer), device_id_type=pl.DeviceIdType.MESH)

    pick = lax.broadcasted_iota(jnp.int32, (plan.table, rows), 0) == index_ref[...]
    pick_ref[...] = pick.astype(F32).astype(BF16)
    local = jnp.zeros((2, rows), F32)
    for piece in pieces(coords_ref[...]):
        local = local + jnp.dot(piece.astype(BF16), pick_ref[...], preferred_element_type=F32)
    xy_ref[me] = local
    pl.semaphore_wait(barrier, len(peers))
    copies = []
    for k, peer in enumerate(flat):
        copies.append(send(xy_ref.at[me], xy_ref.at[me], xy_sem, (k,), at(*peer)))
        copies[-1].start()

    lane = lax.broadcasted_iota(jnp.int32, (share, plan.lats), 1)
    chosen = lane == lax.broadcasted_iota(jnp.int32, (share, plan.lats), 0) + owner * share
    length = jnp.sum(jnp.where(chosen, length_ref[...], 0.0), axis=1, keepdims=True)
    height = jnp.sum(jnp.where(chosen, height_ref[...], 0.0), axis=1, keepdims=True)
    loads[0].wait()
    loads[1].wait()
    point_features(plan, (0.5 * LOG2E) / (length * length), points_ref, weight_ref, table_ref)
    for copy in copies:
        copy.wait()
    cell_features(plan, xy_ref, side_ref, feat_ref)

    def forward(i, carry):
        j, block = i // plan.blocks, lax.rem(i, plan.blocks)
        feat = feat_ref[pl.ds(pl.multiple_of(block * rows, rows), rows), :]
        total = jnp.zeros((rows, 128), F32)
        for start in range(0, plan.points, plan.tile):
            part = table_ref[j, :, start : start + plan.tile].astype(BF16)
            value = jnp.exp2(jnp.dot(feat, part, preferred_element_type=F32))
            for first in range(0, plan.tile, 128):
                w = table_ref[j, SPARE : SPARE + 1, start + first : start + first + 128]
                total = total + value[:, first : first + 128] * w
        wide_ref[i] = total
        return carry

    lax.fori_loop(0, share * plan.blocks, forward, 0)
    for block in range(plan.blocks):
        for j in range(share):
            row = jnp.sum(wide_ref[j * plan.blocks + block].T, axis=0, keepdims=True)
            part_ref[block % subs, block // subs, j : j + 1, :] = row * height[j : j + 1, :]

    copies = []
    for ds in range(1, subs):
        copies.append(send(part_ref.at[lax.rem(s + ds, subs)], near_ref.at[ds - 1], near_sem, (ds - 1,), at(ds=ds)))
        copies[-1].start()
    value = part_ref[s]
    for ds in range(1, subs):
        copies[ds - 1].wait()
        value = value + near_ref[ds - 1]
    final_ref[...] = value.astype(final_ref.dtype)
    copies = []
    for k, peer in enumerate(far):
        target = at(*peer)
        source = final_ref.at[target["lat"] if lats > 1 else 0]
        copies.append(send(source, latent_recv.at[g, l], latent_sem, (k,), target))
        copies[-1].start()
    latent_recv[g, l] = final_ref[l]
    loads[2].wait()
    loads[3].wait()
    loads[4].wait()
    gene_tiles = plan.genes // plan.wide

    def gene_tile(i):
        return pl.ds(pl.multiple_of(i * plan.wide, 128), plan.wide)

    def observe(i, carry):
        cols = gene_tile(i)
        seen = lax.dot_general(
            pick_ref[...], expr_ref[:, cols], (((0,), (0,)), ((), ())), preferred_element_type=F32
        )
        seen_ref[:, cols] = seen.astype(BF16)
        return carry

    lax.fori_loop(0, gene_tiles, observe, 0)
    for copy in copies:
        copy.wait()
    for lat in range(lats):
        for own in range(plan.owners):
            first = own * plan.split
            value = latent_recv[first, lat].astype(F32)
            for other in range(1, plan.split):
                value = value + latent_recv[first + other, lat].astype(F32)
            base = lat * plan.lats + own * share
            side_lat_ref[base : base + share, :] = value
    latent_ref[...] = side_lat_ref[...].astype(BF16)
    turned = side_lat_ref[...].T.astype(BF16)
    cell_ref[...] = jnp.zeros_like(cell_ref)

    def middle(i, carry):
        cols = gene_tile(i)
        mixing = mixing_ref[:, cols]
        predicted = jnp.dot(turned, mixing, preferred_element_type=F32)
        weighted = (noise_ref[:, cols] * (seen_ref[:, cols].astype(F32) - predicted)).astype(BF16)
        seen_ref[:, cols] = weighted
        cell_ref[...] += lax.dot_general(
            mixing, weighted, (((1,), (1,)), ((), ())), preferred_element_type=F32
        )
        return carry

    lax.fori_loop(0, gene_tiles, middle, 0)
    for own in range(plan.owners):
        for lat in range(lats):
            base = lat * plan.lats + own * share
            chunk_ref[own, lat] = plan.scale * cell_ref[base : base + share, :]

    copies = []
    for dg in range(1, genes):
        target = at(dg=dg)
        copies.append(
            send(chunk_ref.at[target["gene"] // plan.split], rs_ref.at[dg - 1], rs_sem, (dg - 1,), target)
        )
        copies[-1].start()

    def mix(i, carry):
        cols = gene_tile(i)
        value = plan.scale * jnp.dot(latent_ref[...], seen_ref[:, cols], preferred_element_type=F32)
        depth = mix_ref.shape[2]
        for sub in range(subs):
            for lat in range(lats):
                base = (sub * lats + lat) * depth
                mix_ref[sub, lat, :, cols] = value[base : base + depth, :]
        return carry

    lax.fori_loop(0, gene_tiles, mix, 0)
    value = chunk_ref[owner]
    for dg in range(1, genes):
        copies[dg - 1].wait()
        value = value + rs_ref[dg - 1]
    own_ref[...] = value
    copies = []
    for k, peer in enumerate(flat):
        target = at(*peer)
        source = own_ref.at[target["lat"] if lats > 1 else 0]
        copies.append(send(source, lg_ref.at[me], lg_sem, (k,), target))
        copies[-1].start()
    lg_ref[me] = own_ref[l]

    near = []
    for ds in range(1, subs):
        near.append(
            send(mix_ref.at[lax.rem(s + ds, subs)], mix_near.at[ds - 1], mix_sem, (0, ds - 1), at(ds=ds))
        )
        near[-1].start()
    scatter = [
        send(mix_two.at[lax.rem(l + dl, lats)], mix_far.at[dl - 1], mix_sem, (1, dl - 1), at(dl=dl))
        for dl in range(1, lats)
    ]
    gather = [send(mix_out.at[s, l], mix_out.at[s, l], mix_sem, (2, dl - 1), at(dl=dl)) for dl in range(1, lats)]
    back = [send(mix_out.at[s], mix_out.at[s], mix_sem, (3, ds - 1), at(ds=ds)) for ds in range(1, subs)]

    def stage_one():
        for ds in range(1, subs):
            near[ds - 1].wait()
        value = mix_ref[s]
        for ds in range(1, subs):
            value = value + mix_near[ds - 1]
        mix_two[...] = value
        for copy in scatter:
            copy.start()

    def stage_two():
        for copy in scatter:
            copy.wait()
        value = mix_two[l]
        for dl in range(1, lats):
            value = value + mix_far[dl - 1]
        mix_out[s, l] = value
        for copy in gather:
            copy.start()

    def stage_three():
        for copy in gather:
            copy.wait()
        for copy in back:
            copy.start()

    for copy in copies:
        copy.wait()
    if share < 8:
        lgpad_ref[...] = jnp.zeros_like(lgpad_ref)
    for block in range(plan.blocks):
        lgpad_ref[:share, :] = lg_ref[block] * height
        columns = lgpad_ref[...].T
        for j in range(share):
            wide_ref[j * plan.blocks + block] = jnp.broadcast_to(columns[:, j : j + 1], (rows, 128))

    stages = {0: stage_one, (3 * share) // 8: stage_two, (6 * share) // 8: stage_three}
    loose = [stage_one, stage_two, stage_three] if len(stages) < 3 else []

    def gather_copy(j, dg):
        return send(all_ref.at[g, j], all_ref.at[g, j], all_sem, (j, dg - 1), at(dg=dg))

    def backward(j, carry):
        if not loose:
            for when, stage in stages.items():
                pl.when(j == when)(stage)
        sum_ref[...] = jnp.zeros_like(sum_ref)

        def products(block, inner):
            feat = feat_ref[pl.ds(pl.multiple_of(block * rows, rows), rows), :]
            at_row = j * plan.blocks + block
            for start in range(0, plan.points, plan.tile):
                part = table_ref[j, :, start : start + plan.tile].astype(BF16)
                value = jnp.exp2(jnp.dot(feat, part, preferred_element_type=F32))
                for first in range(0, plan.tile, 128):
                    term = value[:, first : first + 128] * wide_ref[at_row]
                    sum_ref[:, start + first : start + first + 128] += jnp.sum(
                        term.reshape(rows // 8, 8, 128), axis=0
                    )
            return inner

        lax.fori_loop(0, plan.blocks, products, 0)
        for r in range(plan.points // 128):
            all_ref[g, j, r : r + 1, :] = jnp.sum(sum_ref[:, r * 128 : (r + 1) * 128], axis=0, keepdims=True)
        for dg in range(1, genes):
            gather_copy(j, dg).start()
        return carry

    lax.fori_loop(0, share, backward, 0)
    for stage in loose:
        stage()

    def finish(j, carry):
        for dg in range(1, genes):
            gather_copy(j, dg).wait()
        return carry

    lax.fori_loop(0, share, finish, 0)
    for gene in range(genes):
        base, cut = gene // plan.split * share, gene % plan.split * plan.points
        for r in range(plan.points // 128):
            first = cut + r * 128
            ind_out[base : base + share, first : first + 128] = all_ref[gene, :, r, :]
    for copy in back:
        copy.wait()


def fused(plan, *args):
    genes, lats, subs = plan.gene, plan.lat, plan.sub
    rows, share, blocks = plan.rows, plan.share, plan.blocks
    depth = plan.total // (lats * subs)
    sent = BF16 if plan.split == 1 else F32
    dma = pltpu.SemaphoreType.DMA
    far = genes * lats - 1
    flat = blocks - 1
    vmem = pl.BlockSpec(memory_space=pltpu.VMEM)
    anywhere = pl.BlockSpec(memory_space=pl.ANY)
    scratch = [
        pltpu.VMEM((plan.table, plan.genes), BF16),
        pltpu.VMEM((2, share, plan.points), F32),
        pltpu.VMEM((share, plan.points), F32),
        pltpu.VMEM((plan.total, plan.genes), BF16),
        pltpu.VMEM((1, plan.genes), F32),
        pltpu.VMEM((plan.table, rows), BF16),
        pltpu.VMEM((blocks, 2, rows), F32),
        pltpu.VMEM((128, rows), F32),
        pltpu.VMEM((blocks * rows, DEPTH), BF16),
        pltpu.VMEM((share, DEPTH, plan.points), F32),
        pltpu.VMEM((share * blocks, rows, 128), F32),
        pltpu.VMEM((subs, lats, share, rows), F32),
        pltpu.VMEM((max(1, subs - 1), lats, share, rows), F32),
        pltpu.VMEM((lats, share, rows), sent),
        pltpu.VMEM((genes, lats, share, rows), sent),
        pltpu.VMEM((plan.total, rows), BF16),
        pltpu.VMEM((plan.total, rows), F32),
        pltpu.VMEM((rows, plan.genes), BF16),
        pltpu.VMEM((plan.total, rows), F32),
        pltpu.VMEM((plan.owners, lats, share, rows), F32),
        pltpu.VMEM((max(1, genes - 1), lats, share, rows), F32),
        pltpu.VMEM((lats, share, rows), F32),
        pltpu.VMEM((blocks, share, rows), F32),
        pltpu.VMEM((max(8, share), rows), F32),
        pltpu.VMEM((subs, lats, depth, plan.genes), F32),
        pltpu.VMEM((max(1, subs - 1), lats, depth, plan.genes), F32),
        pltpu.VMEM((max(1, lats - 1), depth, plan.genes), F32),
        pltpu.VMEM((lats, depth, plan.genes), F32),
        pltpu.VMEM((8, plan.points), F32),
        pltpu.VMEM((genes, share, plan.points // 128, 128), F32),
        dma((5,)),
        dma((2, max(1, flat))),
        dma((2, max(1, subs - 1))),
        dma((2, max(1, far))),
        dma((2, max(1, genes - 1))),
        dma((2, max(1, flat))),
        dma((2, 4, max(1, subs - 1, lats - 1))),
        dma((2, share, max(1, genes - 1))),
    ]
    return pl.pallas_call(
        functools.partial(body, plan),
        in_specs=[vmem] * 4 + [anywhere] * 5,
        out_specs=[vmem, vmem],
        out_shape=[
            jax.ShapeDtypeStruct((subs, lats, depth, plan.genes), F32),
            jax.ShapeDtypeStruct((plan.lats, plan.count), F32),
        ],
        scratch_shapes=scratch,
        compiler_params=pltpu.CompilerParams(
            collective_id=0, has_side_effects=True, vmem_limit_bytes=60 * 2**20
        ),
    )(*args)


def on_device(
    cell_index,
    coords_table,
    expr_table,
    inducing,
    ind_weights,
    lengthscale,
    variance,
    mixing,
    noise_prec,
):
    genes, lats, subs = (lax.axis_size(axis) for axis in ("gene", "lat", "sub"))
    latents, count = ind_weights.shape
    owners = math.gcd(genes, latents)
    split = genes // owners
    share = latents // owners
    plan = Plan(
        gene=genes,
        lat=lats,
        sub=subs,
        rows=cell_index.shape[0],
        table=coords_table.shape[1],
        lats=latents,
        count=count,
        genes=expr_table.shape[1],
        share=share,
        split=split,
        sliced=share % 8 != 0,
        scale=-1.0 / math.sqrt(cell_index.shape[0] * lats * subs),
    )
    if plan.sliced:
        place = lax.axis_index("gene")
        first, cut = place // split * share, lax.rem(place, split) * plan.points
        inducing = lax.dynamic_slice(inducing, (0, first, cut), (2, share, plan.points))
        ind_weights = lax.dynamic_slice(ind_weights, (first, cut), (share, plan.points))
    grad_mixing, grad_inducing = fused(
        plan,
        cell_index[None, :],
        coords_table,
        lengthscale[None, :],
        variance[None, :],
        expr_table,
        inducing,
        ind_weights,
        mixing,
        noise_prec[None, :],
    )
    return grad_mixing.reshape(mixing.shape), grad_inducing


def solution(mesh):
    in_specs = (
        P(("group", "lat", "sub")),
        P("group", ("lat", "sub")),
        P(("group", "lat", "sub"), "gene"),
        P("group", "lat", "sub"),
        P(("group", "lat"), "sub"),
        P(("group", "lat")),
        P(("group", "lat")),
        P("group", "gene"),
        P(("group", "gene")),
    )
    out_specs = (P("group", "gene"), P(("group", "lat"), "sub"))
    return jax.shard_map(
        on_device, mesh=mesh, in_specs=in_specs, out_specs=out_specs, check_vma=False
    )
```

time: 151 us -> 80.8 us (0.54)
  Pallas kernels: 115 us -> 75.8 us
  between operations: 14.2 us -> 0.64 us
  local copies, waits for them, and re-layouts: 12.2 us -> 4.14 us
  blocking collectives: 6.01 us -> 0 us
  other arithmetic: 1.75 us -> 0 us
    pallas_call x6 -> x1, Pallas kernels: 115 us -> 75.8 us  [fused(): pl.pallas_call(functools.partial(body, plan), in_specs=[vmem] * 4 + [anyw...]
    all_gather x1 -> x0, blocking collectives: 6.01 us -> none  [on_device(): kernel_xy = lax.all_gather(local_xy, ('lat', 'sub'), axis=1, tiled=True)]
    unnamed x23 -> x2, local copies, waits for them, and re-layouts: 9.65 us -> 4.14 us
    broadcast_in_dim x3 -> x0, local copies, waits for them, and re-layouts: 1.6 us -> none  [the longest x1 0.74 us: products(): length[:, None]]
  transfers between devices with their start and end apart: 1 -> 0, of which waited for: 0 -> 0; matrix products, arithmetic and copies ran while one was open for 0% -> 0% of each run, Pallas kernels for 45% -> 0%
where the time goes in v1:
time: 80.8 us; the launch traced here: 80.5 us
  Pallas kernels  75.8 us (94%)
  local copies, waits for them, and re-layouts  4.14 us (5%)
    pallas_call x1, Pallas kernels, fused(): pl.pallas_call(functools.partial(body, plan), in_specs=[vmem] * 4 + [anyw...  75.8 us
    unnamed x2, local copies, waits for them, and re-layouts  4.14 us

profile of v1, /device:TPU:0, one launch (start us, length us, event | category | flops | bytes accessed | tf_op | source)
XLA Modules:
  0.0 80.5 jit_solution(17160070830281598992)
XLA Ops:
  0.6 75.8 %shard_map.104 = (f32[2,2,16,4096]{3,2,1,0:T(8,128)}, f32[32,4096]{1,0:T(8,128)}) custom-call(s32[1,256]{1,0:T(1,128)} %bitcast.7, f32[2,512]{1,0:T(2,128)} %coords_ref.1, f32[1,32]{1,0:T(1,128)} %bitcast.8, f32[1,32]{1,0:T(1,128)} %bitcast.9, bf16[512,4096]{1,0:T(8,128)(2,1)} %expr_hbm.1, f32[2,32,4096]{2,1,0:T(8,128)} %points_hbm.1, ...), custom_call_target="tpu_custom_call" | custom-call | tf_op jit(solution)/shard_map/pallas_call | solution.py:493
  76.4 2.3 %copy.13 = f32[64,4096]{1,0:T(8,128)} copy(f32[64,4096]{1,0:T(8,128)} %bitcast.5) | data formatting | bytes 2097152
  78.7 1.9 %copy.14 = f32[32,4096]{1,0:T(8,128)} copy(f32[32,4096]{1,0:T(8,128)} %get-tuple-element.9) | data formatting | bytes 1048576

commit v2 on v1

v2 whole, which is shorter than its diff:
```python
import functools
import math
from typing import NamedTuple

import jax
import jax.numpy as jnp
from jax import lax
from jax.experimental import pallas as pl
from jax.experimental.pallas import tpu as pltpu
from jax.sharding import PartitionSpec as P

F32 = jnp.float32
BF16 = jnp.bfloat16
DEPTH = 24
SPARE = 21
CENTER = 0.5
LOG2E = math.log2(math.e)
LEFT = (0, 0, 1, 1, 0, 2)
RIGHT = (0, 1, 0, 1, 2, 0)


class Plan(NamedTuple):
    gene: int
    lat: int
    sub: int
    rows: int
    table: int
    lats: int
    count: int
    genes: int
    share: int
    split: int
    sliced: bool
    scale: float

    @property
    def blocks(self):
        return self.lat * self.sub

    @property
    def points(self):
        return self.count // self.split

    @property
    def owners(self):
        return self.gene // self.split

    @property
    def total(self):
        return self.lat * self.lats

    @property
    def half(self):
        return self.rows // 2

    @property
    def turned(self):
        return -(-3 * self.share // 8) * 8

    @property
    def tile(self):
        return min(256, self.points)

    @property
    def wide(self):
        return min(512, self.genes)


def pieces(value):
    high = value.astype(BF16).astype(F32)
    rest = value - high
    middle = rest.astype(BF16).astype(F32)
    low = (rest - middle).astype(BF16).astype(F32)
    return high, middle, low


def point_features(plan, scale, points_ref, weight_ref, table_ref):
    step = min(512, plan.points)

    def part(i, carry):
        cols = pl.ds(pl.multiple_of(i * step, 128), step)
        x = points_ref[0, :, cols] - CENTER
        y = points_ref[1, :, cols] - CENTER
        px = pieces(x * (2.0 * scale))
        py = pieces(y * (2.0 * scale))
        ps = pieces(jnp.broadcast_to(-scale, x.shape))
        pn = pieces((x * x + y * y) * -scale)
        rows = [px[k] for k in RIGHT] + [py[k] for k in RIGHT] + [ps[k] for k in RIGHT]
        rows += list(pn) + [weight_ref[:, cols]] + [jnp.zeros_like(x)] * (DEPTH - SPARE - 1)
        for place, row in enumerate(rows):
            for lane in range(plan.share):
                table_ref[lane, place : place + 1, cols] = row[lane : lane + 1, :]
        return carry

    lax.fori_loop(0, plan.points // step, part, 0)


def cell_features(plan, block, xy_ref, side_ref, feat_ref):
    x = xy_ref[block, 0:1, :] - CENTER
    y = xy_ref[block, 1:2, :] - CENTER
    px, py, pn = pieces(x), pieces(y), pieces(x * x + y * y)
    rows = [px[k] for k in LEFT] + [py[k] for k in LEFT] + [pn[k] for k in LEFT]
    for place, row in enumerate(rows):
        side_ref[place : place + 1, :] = row
    place = pl.ds(pl.multiple_of(block * plan.rows, plan.rows), plan.rows)
    feat_ref[place, :] = side_ref[...].T[:, :DEPTH].astype(BF16)


def body(
    plan,
    index_ref,
    coords_ref,
    length_ref,
    height_ref,
    expr_hbm,
    points_hbm,
    weight_hbm,
    mixing_hbm,
    noise_hbm,
    mix_out,
    ind_out,
    expr_ref,
    points_ref,
    weight_ref,
    mixing_ref,
    noise_ref,
    pick_ref,
    xy_ref,
    side_ref,
    feat_ref,
    table_ref,
    total_ref,
    part_ref,
    near_ref,
    final_ref,
    latent_recv,
    latent_ref,
    side_lat_ref,
    seen_ref,
    cell_ref,
    chunk_ref,
    rs_ref,
    own_ref,
    lg_ref,
    lgside_ref,
    lgt_ref,
    wide_ref,
    mix_ref,
    mix_near,
    mix_all,
    sum_ref,
    all_ref,
    load_sem,
    xy_sem,
    near_sem,
    latent_sem,
    rs_sem,
    lg_sem,
    mix_sem,
    all_sem,
):
    genes, lats, subs, blocks = plan.gene, plan.lat, plan.sub, plan.blocks
    rows, half, share = plan.rows, plan.half, plan.share
    g, l, s = lax.axis_index("gene"), lax.axis_index("lat"), lax.axis_index("sub")
    owner, slab = g // plan.split, lax.rem(g, plan.split)
    me = l * subs + s

    def at(dg=0, dl=0, ds=0):
        return {"gene": lax.rem(g + dg, genes), "lat": lax.rem(l + dl, lats), "sub": lax.rem(s + ds, subs)}

    def send(src, dst, sems, k, device):
        return pltpu.make_async_remote_copy(
            src_ref=src,
            dst_ref=dst,
            send_sem=sems.at[(0, *k)],
            recv_sem=sems.at[(1, *k)],
            device_id=device,
            device_id_type=pl.DeviceIdType.MESH,
        )

    if plan.sliced:
        points_src, weight_src = points_hbm, weight_hbm
    else:
        mine = pl.ds(pl.multiple_of(owner * share, 8), share)
        cut = pl.ds(pl.multiple_of(slab * plan.points, 128), plan.points)
        points_src, weight_src = points_hbm.at[:, mine, cut], weight_hbm.at[mine, cut]
    loads = [
        pltpu.make_async_copy(points_src, points_ref, load_sem.at[0]),
        pltpu.make_async_copy(weight_src, weight_ref, load_sem.at[1]),
        pltpu.make_async_copy(expr_hbm, expr_ref, load_sem.at[2]),
        pltpu.make_async_copy(mixing_hbm, mixing_ref, load_sem.at[3]),
        pltpu.make_async_copy(noise_hbm, noise_ref, load_sem.at[4]),
    ]
    for load in loads:
        load.start()

    far = [(dg, dl, 0) for dg in range(genes) for dl in range(lats) if dg or dl]
    flat = [(0, dl, ds) for dl in range(lats) for ds in range(subs) if dl or ds]
    peers = sorted(set(far) | set(flat))
    barrier = pltpu.get_barrier_semaphore()
    for peer in peers:
        pl.semaphore_signal(barrier, inc=1, device_id=at(*peer), device_id_type=pl.DeviceIdType.MESH)

    pick = lax.broadcasted_iota(jnp.int32, (plan.table, rows), 0) == index_ref[...]
    pick_ref[...] = pick.astype(F32).astype(BF16)
    local = jnp.zeros((2, rows), F32)
    for piece in pieces(coords_ref[...]):
        local = local + jnp.dot(piece.astype(BF16), pick_ref[...], preferred_element_type=F32)
    xy_ref[me] = local
    side_ref[...] = jnp.zeros_like(side_ref)
    side_ref[18:21, :] = jnp.ones((3, rows), F32)
    cell_features(plan, me, xy_ref, side_ref, feat_ref)

    lane = lax.broadcasted_iota(jnp.int32, (share, plan.lats), 1)
    chosen = lane == lax.broadcasted_iota(jnp.int32, (share, plan.lats), 0) + owner * share
    length = jnp.sum(jnp.where(chosen, length_ref[...], 0.0), axis=1, keepdims=True)
    height = jnp.sum(jnp.where(chosen, height_ref[...], 0.0), axis=1, keepdims=True)
    loads[0].wait()
    loads[1].wait()
    point_features(plan, (0.5 * LOG2E) / (length * length), points_ref, weight_ref, table_ref)

    def ring(k):
        return lax.rem(me + k, blocks)

    one = jnp.ones((8, 128), BF16)

    def flush(j, units):
        for u, (block, part) in enumerate(units):
            row = jnp.zeros((8, half), F32)
            for piece in pieces(total_ref[u]):
                row = row + lax.dot_general(
                    one, piece.astype(BF16), (((1,), (1,)), ((), ())), preferred_element_type=F32
                )
            part_ref[part, lax.rem(block, subs), block // subs, pl.ds(j, 1), :] = row[0:1, :]

    def forward(units, stages):
        def step(j, carry):
            for when, stage in stages:
                pl.when(j == when)(stage)
            flush(jnp.maximum(j - 1, 0), units)
            for u, (block, part) in enumerate(units):
                place = pl.multiple_of(block * rows + part * half, half)
                feat = feat_ref[pl.ds(place, half), :]
                total = jnp.zeros((half, 128), F32)
                for start in range(0, plan.points, plan.tile):
                    cols = slice(start, start + plan.tile)
                    value = jnp.exp2(
                        jnp.dot(feat, table_ref[j, :, cols].astype(BF16), preferred_element_type=F32)
                    )
                    for first in range(0, plan.tile, 128):
                        w = table_ref[j, SPARE : SPARE + 1, start + first : start + first + 128]
                        total = total + value[:, first : first + 128] * w
                total_ref[u] = total
            return carry

        total_ref[...] = jnp.zeros_like(total_ref)
        lax.fori_loop(0, share, step, 0)
        flush(share - 1, units)

    forward([(me, 0), (me, 1)], [])

    pl.semaphore_wait(barrier, len(peers))
    copies = []
    for k, peer in enumerate(flat):
        copies.append(send(xy_ref.at[me], xy_ref.at[me], xy_sem, (k,), at(*peer)))
        copies[-1].start()
    for load in loads[2:]:
        load.wait()
    gene_tiles = plan.genes // plan.wide

    def gene_tile(i):
        return pl.ds(pl.multiple_of(i * plan.wide, 128), plan.wide)

    def observe(i, carry):
        cols = gene_tile(i)
        seen = lax.dot_general(
            pick_ref[...], expr_ref[:, cols], (((0,), (0,)), ((), ())), preferred_element_type=F32
        )
        seen_ref[:, cols] = seen.astype(BF16)
        return carry

    lax.fori_loop(0, gene_tiles, observe, 0)
    for copy in copies:
        copy.wait()
    for k in range(1, blocks):
        cell_features(plan, ring(k), xy_ref, side_ref, feat_ref)

    def near_copies(part):
        return [
            send(part_ref.at[part, lax.rem(s + ds, subs)], near_ref.at[part, ds - 1], near_sem, (part, ds - 1), at(ds=ds))
            for ds in range(1, subs)
        ]

    def latent_copies(part):
        out = []
        for k, peer in enumerate(far):
            target = at(*peer)
            out.append(
                send(final_ref.at[part, target["lat"]], latent_recv.at[part, g, l], latent_sem, (part, k), target)
            )
        return out

    def rs_copies(part):
        out = []
        for dg in range(1, genes):
            target = at(dg=dg)
            source = chunk_ref.at[part, target["gene"] // plan.split]
            out.append(send(source, rs_ref.at[part, dg - 1], rs_sem, (part, dg - 1), target))
        return out

    def lg_copies(part):
        out = []
        for k, peer in enumerate(flat):
            target = at(*peer)
            out.append(send(own_ref.at[part, target["lat"]], lg_ref.at[part, me], lg_sem, (part, k), target))
        return out

    def start(copies):
        for copy in copies:
            copy.start()

    def wait(copies):
        for copy in copies:
            copy.wait()

    def sum_near(part):
        wait(near_copies(part))
        value = part_ref[part, s]
        for ds in range(1, subs):
            value = value + near_ref[part, ds - 1]
        value = value * height[None]
        final_ref[part] = value.astype(final_ref.dtype)
        start(latent_copies(part))
        latent_recv[part, g, l] = final_ref[part, l]

    def middle(part):
        wait(latent_copies(part))
        for lat in range(lats):
            for own in range(plan.owners):
                first = own * plan.split
                value = latent_recv[part, first, lat].astype(F32)
                for other in range(1, plan.split):
                    value = value + latent_recv[part, first + other, lat].astype(F32)
                base = lat * plan.lats + own * share
                side_lat_ref[base : base + share, :] = value
        cells = slice(part * half, (part + 1) * half)
        latent_ref[:, cells] = side_lat_ref[...].astype(BF16)
        turned = side_lat_ref[...].T.astype(BF16)
        cell_ref[...] = jnp.zeros_like(cell_ref)

        def tile(i, carry):
            cols = gene_tile(i)
            mixing = mixing_ref[:, cols]
            predicted = jnp.dot(turned, mixing, preferred_element_type=F32)
            weighted = (noise_ref[:, cols] * (seen_ref[cells, cols].astype(F32) - predicted)).astype(BF16)
            seen_ref[cells, cols] = weighted
            cell_ref[...] += lax.dot_general(
                mixing, weighted, (((1,), (1,)), ((), ())), preferred_element_type=F32
            )
            return carry

        lax.fori_loop(0, gene_tiles, tile, 0)
        for own in range(plan.owners):
            for lat in range(lats):
                base = lat * plan.lats + own * share
                chunk_ref[part, own, lat] = plan.scale * cell_ref[base : base + share, :]
        start(rs_copies(part))

    def sum_gene(part):
        wait(rs_copies(part))
        value = chunk_ref[part, owner]
        for dg in range(1, genes):
            value = value + rs_ref[part, dg - 1]
        own_ref[part] = value
        start(lg_copies(part))
        lg_ref[part, me] = own_ref[part, l]

    def turn(part):
        wait(lg_copies(part))
        for block in range(blocks):
            for p, piece in enumerate(pieces(lg_ref[part, block] * height)):
                lgside_ref[p * share : (p + 1) * share, :] = piece
            lgt_ref[block * half : (block + 1) * half, :] = (
                lgside_ref[...].T[:, : plan.turned].astype(BF16)
            )

    def mix_near_copies():
        return [
            send(mix_ref.at[lax.rem(s + ds, subs)], mix_near.at[ds - 1], mix_sem, (0, ds - 1, 0), at(ds=ds))
            for ds in range(1, subs)
        ]

    def mix_lat_copies(p):
        return [send(mix_all.at[l, p], mix_all.at[l, p], mix_sem, (1, dl - 1, p), at(dl=dl)) for dl in range(1, lats)]

    def mix_back_copies(p):
        return [send(mix_out.at[s, p], mix_out.at[s, p], mix_sem, (2, ds - 1, p), at(ds=ds)) for ds in range(1, subs)]

    def mix_part():
        def tile(i, carry):
            cols = gene_tile(i)
            value = plan.scale * jnp.dot(latent_ref[...], seen_ref[:, cols], preferred_element_type=F32)
            depth = mix_ref.shape[2]
            for sub in range(subs):
                for p in range(lats):
                    base = (sub * lats + p) * depth
                    mix_ref[sub, p, :, cols] = value[base : base + depth, :]
            return carry

        lax.fori_loop(0, gene_tiles, tile, 0)
        start(mix_near_copies())

    def mix_sub():
        wait(mix_near_copies())
        for p in range(lats):
            value = mix_ref[s, p]
            for ds in range(1, subs):
                value = value + mix_near[ds - 1, p]
            mix_all[l, p] = value
            start(mix_lat_copies(p))

    def mix_lat(p):
        wait(mix_lat_copies(p))
        value = mix_all[0, p]
        for lat in range(1, lats):
            value = value + mix_all[lat, p]
        mix_out[s, p] = value
        start(mix_back_copies(p))

    def gather_copies(j):
        return [
            send(all_ref.at[g, j], all_ref.at[g, j], all_sem, (j, dg - 1), at(dg=dg)) for dg in range(1, genes)
        ]

    def backward(part, stages):
        def step(j, carry):
            for when, stage in stages:
                pl.when(j == when)(stage)
            row = lax.broadcasted_iota(jnp.int32, (plan.turned, 128), 0)
            select = (lax.rem(row, share) == j).astype(F32).astype(BF16)
            for block in range(blocks):
                turned = lgt_ref[block * half : (block + 1) * half, :]
                wide_ref[block] = jnp.dot(turned, select, preferred_element_type=F32)
            for start_ in range(0, plan.points, plan.tile):
                cols = slice(start_, start_ + plan.tile)
                points = table_ref[j, :, cols].astype(BF16)
                sums = [None] * (plan.tile // 128)
                for block in range(blocks):
                    feat = feat_ref[block * rows + part * half : block * rows + (part + 1) * half, :]
                    value = jnp.exp2(jnp.dot(feat, points, preferred_element_type=F32))
                    for f in range(plan.tile // 128):
                        term = value[:, f * 128 : (f + 1) * 128] * wide_ref[block]
                        term = jnp.sum(term.reshape(half // 8, 8, 128), axis=0)
                        sums[f] = term if sums[f] is None else sums[f] + term
                for f in range(plan.tile // 128):
                    here = slice(start_ + f * 128, start_ + (f + 1) * 128)
                    if part == 0:
                        sum_ref[j, :, here] = sums[f]
                    else:
                        r = start_ // 128 + f
                        all_ref[g, j, r : r + 1, :] = jnp.sum(sum_ref[j, :, here] + sums[f], axis=0, keepdims=True)
            if part == 1:
                start(gather_copies(j))
            return carry

        lax.fori_loop(0, share, step, 0)

    def when(k):
        return k * share // 8

    forward([(ring(k), 0) for k in range(1, blocks)], [])
    start(near_copies(0))
    forward(
        [(ring(k), 1) for k in range(1, blocks)],
        [
            (when(1), lambda: sum_near(0)),
            (when(4), lambda: middle(0)),
            (when(7), lambda: sum_gene(0)),
        ],
    )
    start(near_copies(1))
    lgside_ref[...] = jnp.zeros_like(lgside_ref)
    turn(0)
    backward(
        0,
        [
            (when(1), lambda: sum_near(1)),
            (when(3), lambda: middle(1)),
            (when(3), mix_part),
            (when(6), lambda: sum_gene(1)),
            (when(6), mix_sub),
        ],
    )
    turn(1)
    early = max(1, lats // 2)

    def first_parts():
        for p in range(early):
            mix_lat(p)

    backward(1, [(when(3), first_parts)])
    for p in range(early, lats):
        mix_lat(p)

    def finish(j, carry):
        wait(gather_copies(j))
        return carry

    lax.fori_loop(0, share, finish, 0)
    for gene in range(genes):
        base, cut = gene // plan.split * share, gene % plan.split * plan.points
        for r in range(plan.points // 128):
            first = cut + r * 128
            ind_out[base : base + share, first : first + 128] = all_ref[gene, :, r, :]
    for p in range(lats):
        wait(mix_back_copies(p))


def fused(plan, *args):
    genes, lats, subs = plan.gene, plan.lat, plan.sub
    rows, half, share, blocks = plan.rows, plan.half, plan.share, plan.blocks
    depth = plan.total // (lats * subs)
    sent = BF16 if plan.split == 1 else F32
    dma = pltpu.SemaphoreType.DMA
    far = genes * lats - 1
    flat = blocks - 1
    vmem = pl.BlockSpec(memory_space=pltpu.VMEM)
    anywhere = pl.BlockSpec(memory_space=pl.ANY)
    scratch = [
        pltpu.VMEM((plan.table, plan.genes), BF16),
        pltpu.VMEM((2, share, plan.points), F32),
        pltpu.VMEM((share, plan.points), F32),
        pltpu.VMEM((plan.total, plan.genes), BF16),
        pltpu.VMEM((1, plan.genes), F32),
        pltpu.VMEM((plan.table, rows), BF16),
        pltpu.VMEM((blocks, 2, rows), F32),
        pltpu.VMEM((128, rows), F32),
        pltpu.VMEM((blocks * rows, DEPTH), BF16),
        pltpu.VMEM((share, DEPTH, plan.points), F32),
        pltpu.VMEM((max(2, blocks - 1), half, 128), F32),
        pltpu.VMEM((2, subs, lats, share, half), F32),
        pltpu.VMEM((2, max(1, subs - 1), lats, share, half), F32),
        pltpu.VMEM((2, lats, share, half), sent),
        pltpu.VMEM((2, genes, lats, share, half), sent),
        pltpu.VMEM((plan.total, rows), BF16),
        pltpu.VMEM((plan.total, half), F32),
        pltpu.VMEM((rows, plan.genes), BF16),
        pltpu.VMEM((plan.total, half), F32),
        pltpu.VMEM((2, plan.owners, lats, share, half), F32),
        pltpu.VMEM((2, max(1, genes - 1), lats, share, half), F32),
        pltpu.VMEM((2, lats, share, half), F32),
        pltpu.VMEM((2, blocks, share, half), F32),
        pltpu.VMEM((128, half), F32),
        pltpu.VMEM((blocks * half, plan.turned), BF16),
        pltpu.VMEM((blocks, half, 128), F32),
        pltpu.VMEM((subs, lats, depth, plan.genes), F32),
        pltpu.VMEM((max(1, subs - 1), lats, depth, plan.genes), F32),
        pltpu.VMEM((lats, lats, depth, plan.genes), F32),
        pltpu.VMEM((share, 8, plan.points), F32),
        pltpu.VMEM((genes, share, plan.points // 128, 128), F32),
        dma((5,)),
        dma((2, max(1, flat))),
        dma((2, 2, max(1, subs - 1))),
        dma((2, 2, max(1, far))),
        dma((2, 2, max(1, genes - 1))),
        dma((2, 2, max(1, flat))),
        dma((2, 3, max(1, subs - 1, lats - 1), lats)),
        dma((2, share, max(1, genes - 1))),
    ]
    return pl.pallas_call(
        functools.partial(body, plan),
        in_specs=[vmem] * 4 + [anywhere] * 5,
        out_specs=[vmem, vmem],
        out_shape=[
            jax.ShapeDtypeStruct((subs, lats, depth, plan.genes), F32),
            jax.ShapeDtypeStruct((plan.lats, plan.count), F32),
        ],
        scratch_shapes=scratch,
        compiler_params=pltpu.CompilerParams(
            collective_id=0, has_side_effects=True, vmem_limit_bytes=60 * 2**20
        ),
    )(*args)


def on_device(
    cell_index,
    coords_table,
    expr_table,
    inducing,
    ind_weights,
    lengthscale,
    variance,
    mixing,
    noise_prec,
):
    genes, lats, subs = (lax.axis_size(axis) for axis in ("gene", "lat", "sub"))
    latents, count = ind_weights.shape
    owners = math.gcd(genes, latents)
    split = genes // owners
    share = latents // owners
    plan = Plan(
        gene=genes,
        lat=lats,
        sub=subs,
        rows=cell_index.shape[0],
        table=coords_table.shape[1],
        lats=latents,
        count=count,
        genes=expr_table.shape[1],
        share=share,
        split=split,
        sliced=share % 8 != 0,
        scale=-1.0 / math.sqrt(cell_index.shape[0] * lats * subs),
    )
    if plan.sliced:
        place = lax.axis_index("gene")
        first, cut = place // split * share, lax.rem(place, split) * plan.points
        inducing = lax.dynamic_slice(inducing, (0, first, cut), (2, share, plan.points))
        ind_weights = lax.dynamic_slice(ind_weights, (first, cut), (share, plan.points))
    grad_mixing, grad_inducing = fused(
        plan,
        cell_index[None, :],
        coords_table,
        lengthscale[None, :],
        variance[None, :],
        expr_table,
        inducing,
        ind_weights,
        mixing,
        noise_prec[None, :],
    )
    return grad_mixing.reshape(mixing.shape), grad_inducing


def solution(mesh):
    in_specs = (
        P(("group", "lat", "sub")),
        P("group", ("lat", "sub")),
        P(("group", "lat", "sub"), "gene"),
        P("group", "lat", "sub"),
        P(("group", "lat"), "sub"),
        P(("group", "lat")),
        P(("group", "lat")),
        P("group", "gene"),
        P(("group", "gene")),
    )
    out_specs = (P("group", "gene"), P(("group", "lat"), "sub"))
    return jax.shard_map(
        on_device, mesh=mesh, in_specs=in_specs, out_specs=out_specs, check_vma=False
    )
```

time: 80.8 us -> 77.6 us (0.960)
  Pallas kernels: 75.8 us -> 72.6 us
    pallas_call x1, Pallas kernels: 75.8 us -> 72.6 us  [fused(): pl.pallas_call(functools.partial(body, plan), in_specs=[vmem] * 4 + [anyw...]
where the time goes in v2:
time: 77.6 us; the launch traced here: 77.3 us
  Pallas kernels  72.6 us (94%)
  local copies, waits for them, and re-layouts  4.14 us (5%)
    pallas_call x1, Pallas kernels, fused(): pl.pallas_call(functools.partial(body, plan), in_specs=[vmem] * 4 + [anyw...  72.6 us
    unnamed x2, local copies, waits for them, and re-layouts  4.14 us

profile of v2, /device:TPU:0, one launch (start us, length us, event | category | flops | bytes accessed | tf_op | source)
XLA Modules:
  0.0 77.3 jit_solution(1169918815960640173)
XLA Ops:
  0.6 72.6 %shard_map.104 = (f32[2,2,16,4096]{3,2,1,0:T(8,128)}, f32[32,4096]{1,0:T(8,128)}) custom-call(s32[1,256]{1,0:T(1,128)} %bitcast.7, f32[2,512]{1,0:T(2,128)} %coords_ref.1, f32[1,32]{1,0:T(1,128)} %bitcast.8, f32[1,32]{1,0:T(1,128)} %bitcast.9, bf16[512,4096]{1,0:T(8,128)(2,1)} %expr_hbm.1, f32[2,32,4096]{2,1,0:T(8,128)} %points_hbm.1, ...), custom_call_target="tpu_custom_call" | custom-call | tf_op jit(solution)/shard_map/pallas_call | solution.py:570
  73.2 2.3 %copy.13 = f32[64,4096]{1,0:T(8,128)} copy(f32[64,4096]{1,0:T(8,128)} %bitcast.5) | data formatting | bytes 2097152
  75.5 1.9 %copy.14 = f32[32,4096]{1,0:T(8,128)} copy(f32[32,4096]{1,0:T(8,128)} %get-tuple-element.9) | data formatting | bytes 1048576

commit v3 on v2

--- a/solution.py
+++ b/solution.py
@@ -118,7 +118,7 @@
     mixing_hbm,
     noise_hbm,
     mix_out,
-    ind_out,
+    all_out,
     expr_ref,
     points_ref,
     weight_ref,
@@ -148,6 +148,7 @@
     mix_ref,
     mix_near,
     mix_all,
+    mix_sum,
     sum_ref,
     all_ref,
     load_sem,
@@ -158,6 +159,7 @@
     lg_sem,
     mix_sem,
     all_sem,
+    keep_sem,
 ):
     genes, lats, subs, blocks = plan.gene, plan.lat, plan.sub, plan.blocks
     rows, half, share = plan.rows, plan.half, plan.share
@@ -191,7 +193,7 @@
         pltpu.make_async_copy(mixing_hbm, mixing_ref, load_sem.at[3]),
         pltpu.make_async_copy(noise_hbm, noise_ref, load_sem.at[4]),
     ]
-    for load in loads:
+    for load in loads[:2]:
         load.start()
 
     far = [(dg, dl, 0) for dg in range(genes) for dl in range(lats) if dg or dl]
@@ -217,29 +219,26 @@
     height = jnp.sum(jnp.where(chosen, height_ref[...], 0.0), axis=1, keepdims=True)
     loads[0].wait()
     loads[1].wait()
+    for load in loads[2:]:
+        load.start()
     point_features(plan, (0.5 * LOG2E) / (length * length), points_ref, weight_ref, table_ref)
 
     def ring(k):
         return lax.rem(me + k, blocks)
 
-    one = jnp.ones((8, 128), BF16)
-
-    def flush(j, units):
-        for u, (block, part) in enumerate(units):
-            row = jnp.zeros((8, half), F32)
-            for piece in pieces(total_ref[u]):
-                row = row + lax.dot_general(
-                    one, piece.astype(BF16), (((1,), (1,)), ((), ())), preferred_element_type=F32
-                )
-            part_ref[part, lax.rem(block, subs), block // subs, pl.ds(j, 1), :] = row[0:1, :]
+    def flush(part):
+        for k in range(blocks):
+            for j in range(share):
+                row = jnp.sum(total_ref[j, 2 * k + part].T, axis=0, keepdims=True)
+                part_ref[part, lax.rem(ring(k), subs), ring(k) // subs, j : j + 1, :] = row
+        start(near_copies(part))
 
     def forward(units, stages):
         def step(j, carry):
             for when, stage in stages:
                 pl.when(j == when)(stage)
-            flush(jnp.maximum(j - 1, 0), units)
-            for u, (block, part) in enumerate(units):
-                place = pl.multiple_of(block * rows + part * half, half)
+            for k, part in units:
+                place = pl.multiple_of(ring(k) * rows + part * half, half)
                 feat = feat_ref[pl.ds(place, half), :]
                 total = jnp.zeros((half, 128), F32)
                 for start in range(0, plan.points, plan.tile):
@@ -250,14 +249,12 @@
                     for first in range(0, plan.tile, 128):
                         w = table_ref[j, SPARE : SPARE + 1, start + first : start + first + 128]
                         total = total + value[:, first : first + 128] * w
-                total_ref[u] = total
+                total_ref[j, 2 * k + part] = total
             return carry
 
-        total_ref[...] = jnp.zeros_like(total_ref)
         lax.fori_loop(0, share, step, 0)
-        flush(share - 1, units)
-
-    forward([(me, 0), (me, 1)], [])
+
+    forward([(0, 0), (0, 1)], [])
 
     pl.semaphore_wait(barrier, len(peers))
     copies = []
@@ -266,20 +263,12 @@
         copies[-1].start()
     for load in loads[2:]:
         load.wait()
-    gene_tiles = plan.genes // plan.wide
-
-    def gene_tile(i):
-        return pl.ds(pl.multiple_of(i * plan.wide, 128), plan.wide)
-
-    def observe(i, carry):
-        cols = gene_tile(i)
+    gene_tiles = [slice(first, first + plan.wide) for first in range(0, plan.genes, plan.wide)]
+    for cols in gene_tiles:
         seen = lax.dot_general(
             pick_ref[...], expr_ref[:, cols], (((0,), (0,)), ((), ())), preferred_element_type=F32
         )
         seen_ref[:, cols] = seen.astype(BF16)
-        return carry
-
-    lax.fori_loop(0, gene_tiles, observe, 0)
     for copy in copies:
         copy.wait()
     for k in range(1, blocks):
@@ -346,20 +335,16 @@
         cells = slice(part * half, (part + 1) * half)
         latent_ref[:, cells] = side_lat_ref[...].astype(BF16)
         turned = side_lat_ref[...].T.astype(BF16)
-        cell_ref[...] = jnp.zeros_like(cell_ref)
-
-        def tile(i, carry):
-            cols = gene_tile(i)
+        cell = jnp.zeros((plan.total, half), F32)
+        for cols in gene_tiles:
             mixing = mixing_ref[:, cols]
             predicted = jnp.dot(turned, mixing, preferred_element_type=F32)
             weighted = (noise_ref[:, cols] * (seen_ref[cells, cols].astype(F32) - predicted)).astype(BF16)
             seen_ref[cells, cols] = weighted
-            cell_ref[...] += lax.dot_general(
+            cell = cell + lax.dot_general(
                 mixing, weighted, (((1,), (1,)), ((), ())), preferred_element_type=F32
             )
-            return carry
-
-        lax.fori_loop(0, gene_tiles, tile, 0)
+        cell_ref[...] = cell
         for own in range(plan.owners):
             for lat in range(lats):
                 base = lat * plan.lats + own * share
@@ -394,20 +379,19 @@
         return [send(mix_all.at[l, p], mix_all.at[l, p], mix_sem, (1, dl - 1, p), at(dl=dl)) for dl in range(1, lats)]
 
     def mix_back_copies(p):
-        return [send(mix_out.at[s, p], mix_out.at[s, p], mix_sem, (2, ds - 1, p), at(ds=ds)) for ds in range(1, subs)]
+        return [send(mix_sum.at[p], mix_out.at[s, p], mix_sem, (2, ds - 1, p), at(ds=ds)) for ds in range(1, subs)]
+
+    def mix_keep(p):
+        return pltpu.make_async_copy(mix_sum.at[p], mix_out.at[s, p], keep_sem.at[p])
 
     def mix_part():
-        def tile(i, carry):
-            cols = gene_tile(i)
+        depth = mix_ref.shape[2]
+        for cols in gene_tiles:
             value = plan.scale * jnp.dot(latent_ref[...], seen_ref[:, cols], preferred_element_type=F32)
-            depth = mix_ref.shape[2]
             for sub in range(subs):
                 for p in range(lats):
                     base = (sub * lats + p) * depth
                     mix_ref[sub, p, :, cols] = value[base : base + depth, :]
-            return carry
-
-        lax.fori_loop(0, gene_tiles, tile, 0)
         start(mix_near_copies())
 
     def mix_sub():
@@ -424,13 +408,15 @@
         value = mix_all[0, p]
         for lat in range(1, lats):
             value = value + mix_all[lat, p]
-        mix_out[s, p] = value
+        mix_sum[p] = value
         start(mix_back_copies(p))
-
-    def gather_copies(j):
+        mix_keep(p).start()
+
+    def gather_copies(j, h):
         return [
-            send(all_ref.at[g, j], all_ref.at[g, j], all_sem, (j, dg - 1), at(dg=dg)) for dg in range(1, genes)
-        ]
+            send(all_ref.at[j, h], all_out.at[g, j, h], all_sem, (j, h, dg - 1), at(dg=dg))
+            for dg in range(1, genes)
+        ] + [pltpu.make_async_copy(all_ref.at[j, h], all_out.at[g, j, h], keep_sem.at[lats + 2 * j + h])]
 
     def backward(part, stages):
         def step(j, carry):
@@ -457,10 +443,14 @@
                     if part == 0:
                         sum_ref[j, :, here] = sums[f]
                     else:
-                        r = start_ // 128 + f
-                        all_ref[g, j, r : r + 1, :] = jnp.sum(sum_ref[j, :, here] + sums[f], axis=0, keepdims=True)
+                        h, r = divmod(start_ // 128 + f, plan.points // 256)
+                        all_ref[j, h, r : r + 1, :] = jnp.sum(sum_ref[j, :, here] + sums[f], axis=0, keepdims=True)
+                if part == 1 and start_ + plan.tile == plan.points // 2:
+                    start(gather_copies(j, 0))
             if part == 1:
-                start(gather_copies(j))
+                if plan.tile > plan.points // 2:
+                    start(gather_copies(j, 0))
+                start(gather_copies(j, 1))
             return carry
 
         lax.fori_loop(0, share, step, 0)
@@ -468,17 +458,17 @@
     def when(k):
         return k * share // 8
 
-    forward([(ring(k), 0) for k in range(1, blocks)], [])
-    start(near_copies(0))
+    forward([(k, 0) for k in range(1, blocks)], [])
+    flush(0)
     forward(
-        [(ring(k), 1) for k in range(1, blocks)],
+        [(k, 1) for k in range(1, blocks)],
         [
             (when(1), lambda: sum_near(0)),
-            (when(4), lambda: middle(0)),
+            (when(5), lambda: middle(0)),
             (when(7), lambda: sum_gene(0)),
         ],
     )
-    start(near_copies(1))
+    flush(1)
     lgside_ref[...] = jnp.zeros_like(lgside_ref)
     turn(0)
     backward(
@@ -498,22 +488,81 @@
         for p in range(early):
             mix_lat(p)
 
-    backward(1, [(when(3), first_parts)])
+    backward(1, [(when(5), first_parts)])
     for p in range(early, lats):
         mix_lat(p)
 
     def finish(j, carry):
-        wait(gather_copies(j))
+        wait(gather_copies(j, 0))
+        wait(gather_copies(j, 1))
         return carry
 
     lax.fori_loop(0, share, finish, 0)
-    for gene in range(genes):
-        base, cut = gene // plan.split * share, gene % plan.split * plan.points
-        for r in range(plan.points // 128):
-            first = cut + r * 128
-            ind_out[base : base + share, first : first + 128] = all_ref[gene, :, r, :]
     for p in range(lats):
         wait(mix_back_copies(p))
+        mix_keep(p).wait()
+
+
+def lay_body(plan, mix_hbm, all_hbm, mix_out, ind_out, mix_ref, all_ref, ind_ref, in_sem, out_sem):
+    subs, lats, depth, _ = mix_hbm.shape
+    parts = [(sub, p) for sub in range(subs) for p in range(lats)]
+    mixes = [
+        pltpu.make_async_copy(mix_hbm.at[sub, p], mix_ref.at[i], in_sem.at[i]) for i, (sub, p) in enumerate(parts)
+    ]
+    outs = [
+        pltpu.make_async_copy(mix_ref.at[i], mix_out.at[pl.ds(i * depth, depth)], out_sem.at[i])
+        for i in range(len(parts))
+    ]
+    whole = pltpu.make_async_copy(all_hbm, all_ref, in_sem.at[len(parts)])
+    whole.start()
+    for copy in mixes:
+        copy.start()
+    whole.wait()
+    last = []
+    half = plan.points // 256
+    for owner in range(plan.owners):
+        base = owner * plan.share
+        for slab in range(plan.split):
+            for r in range(plan.points // 128):
+                first = slab * plan.points + r * 128
+                h, row = divmod(r, half)
+                piece = all_ref[owner * plan.split + slab, :, h, row, :]
+                ind_ref[base : base + plan.share, first : first + 128] = piece
+        if plan.share % 8 == 0:
+            rows = pl.ds(base, plan.share)
+            last.append(pltpu.make_async_copy(ind_ref.at[rows], ind_out.at[rows], out_sem.at[len(parts) + owner]))
+            last[-1].start()
+    if plan.share % 8:
+        last.append(pltpu.make_async_copy(ind_ref, ind_out, out_sem.at[len(parts)]))
+        last[-1].start()
+    for copy, out in zip(mixes, outs):
+        copy.wait()
+        out.start()
+    for copy in outs + last:
+        copy.wait()
+
+
+def lay(plan, mix, all_):
+    subs, lats, depth, genes = mix.shape
+    parts = subs * lats
+    anywhere = pl.BlockSpec(memory_space=pl.ANY)
+    return pl.pallas_call(
+        functools.partial(lay_body, plan),
+        in_specs=[anywhere] * 2,
+        out_specs=[anywhere] * 2,
+        out_shape=[
+            jax.ShapeDtypeStruct((plan.total, genes), F32),
+            jax.ShapeDtypeStruct((plan.lats, plan.count), F32),
+        ],
+        scratch_shapes=[
+            pltpu.VMEM((parts, depth, genes), F32),
+            pltpu.VMEM(all_.shape, F32),
+            pltpu.VMEM((plan.lats, plan.count), F32),
+            pltpu.SemaphoreType.DMA((parts + 1,)),
+            pltpu.SemaphoreType.DMA((parts + plan.owners,)),
+        ],
+        compiler_params=pltpu.CompilerParams(vmem_limit_bytes=16 * 2**20),
+    )(mix, all_)
 
 
 def fused(plan, *args):
@@ -537,7 +586,7 @@
         pltpu.VMEM((128, rows), F32),
         pltpu.VMEM((blocks * rows, DEPTH), BF16),
         pltpu.VMEM((share, DEPTH, plan.points), F32),
-        pltpu.VMEM((max(2, blocks - 1), half, 128), F32),
+        pltpu.VMEM((share, 2 * blocks, half, 128), F32),
         pltpu.VMEM((2, subs, lats, share, half), F32),
         pltpu.VMEM((2, max(1, subs - 1), lats, share, half), F32),
         pltpu.VMEM((2, lats, share, half), sent),
@@ -556,8 +605,9 @@
         pltpu.VMEM((subs, lats, depth, plan.genes), F32),
         pltpu.VMEM((max(1, subs - 1), lats, depth, plan.genes), F32),
         pltpu.VMEM((lats, lats, depth, plan.genes), F32),
+        pltpu.VMEM((lats, depth, plan.genes), F32),
         pltpu.VMEM((share, 8, plan.points), F32),
-        pltpu.VMEM((genes, share, plan.points // 128, 128), F32),
+        pltpu.VMEM((share, 2, plan.points // 256, 128), F32),
         dma((5,)),
         dma((2, max(1, flat))),
         dma((2, 2, max(1, subs - 1))),
@@ -565,15 +615,16 @@
         dma((2, 2, max(1, genes - 1))),
         dma((2, 2, max(1, flat))),
         dma((2, 3, max(1, subs - 1, lats - 1), lats)),
-        dma((2, share, max(1, genes - 1))),
+        dma((2, share, 2, max(1, genes - 1))),
+        dma((lats + 2 * share,)),
     ]
     return pl.pallas_call(
         functools.partial(body, plan),
         in_specs=[vmem] * 4 + [anywhere] * 5,
-        out_specs=[vmem, vmem],
+        out_specs=[anywhere, anywhere],
         out_shape=[
             jax.ShapeDtypeStruct((subs, lats, depth, plan.genes), F32),
-            jax.ShapeDtypeStruct((plan.lats, plan.count), F32),
+            jax.ShapeDtypeStruct((genes, share, 2, plan.points // 256, 128), F32),
         ],
         scratch_shapes=scratch,
         compiler_params=pltpu.CompilerParams(
@@ -617,7 +668,7 @@
         first, cut = place // split * share, lax.rem(place, split) * plan.points
         inducing = lax.dynamic_slice(inducing, (0, first, cut), (2, share, plan.points))
         ind_weights = lax.dynamic_slice(ind_weights, (first, cut), (share, plan.points))
-    grad_mixing, grad_inducing = fused(
+    mix, gathered = fused(
         plan,
         cell_index[None, :],
         coords_table,
@@ -629,7 +680,7 @@
         mixing,
         noise_prec[None, :],
     )
-    return grad_mixing.reshape(mixing.shape), grad_inducing
+    return lay(plan, mix, gathered)
 
 
 def solution(mesh):

time: 77.6 us -> 70 us (0.902)
  Pallas kernels: 72.6 us -> 66.8 us
  local copies, waits for them, and re-layouts: 4.14 us -> 2.26 us
    pallas_call x1, Pallas kernels: 72.6 us -> 65.3 us  [fused(): pl.pallas_call(functools.partial(body, plan), in_specs=[vmem] * 4 + [anyw...]
    unnamed x2 -> x4, local copies, waits for them, and re-layouts: 4.14 us -> 2.26 us
    pallas_call x0 -> x1, Pallas kernels: none -> 1.52 us  [lay(): pl.pallas_call(functools.partial(lay_body, plan), in_specs=[anywhere] * 2...]
where the time goes in v3:
time: 70 us; the launch traced here: 69.7 us
  Pallas kernels  66.8 us (95%)
  local copies, waits for them, and re-layouts  2.26 us (3%)
    pallas_call x1, Pallas kernels, fused(): pl.pallas_call(functools.partial(body, plan), in_specs=[vmem] * 4 + [anyw...  65.3 us
    unnamed x4, local copies, waits for them, and re-layouts  2.26 us
    pallas_call x1, Pallas kernels, lay(): pl.pallas_call(functools.partial(lay_body, plan), in_specs=[anywhere] * 2...  1.52 us

profile of v3, /device:TPU:0, one launch (start us, length us, event | category | flops | bytes accessed | tf_op | source)
XLA Modules:
  0.0 69.7 jit_solution(17415448096769103824)
XLA Ops:
  0.6 65.3 %shard_map.104 = (f32[2,2,16,4096]{3,2,1,0:T(8,128)}, f32[4,8,2,16,128]{4,3,2,1,0:T(8,128)}) custom-call(s32[1,256]{1,0:T(1,128)} %bitcast.5, f32[2,512]{1,0:T(2,128)} %coords_ref.1, f32[1,32]{1,0:T(1,128)} %bitcast.6, f32[1,32]{1,0:T(1,128)} %bitcast.7, bf16[512,4096]{1,0:T(8,128)(2,1)} %expr_hbm.1, f32[2,32,4096]{2,1,0:T(8,128)} %points_hbm.1, ...), custom_call_target="tpu_custom_call" | custom-call | tf_op jit(solution)/shard_map/pallas_call | solution.py:621
  65.9 0.0 copy-start
  65.9 1.2 %copy-done = f32[2,2,16,4096]{3,2,1,0:T(8,128)S(1)} copy-done((f32[2,2,16,4096]{3,2,1,0:T(8,128)S(1)}, f32[2,2,16,4096]{3,2,1,0:T(8,128)}, u32[]{:S(2)}) %copy-start) | copy-done | bytes 1048600
  67.1 0.0 copy-start.1
  67.2 1.0 %copy-done.1 = f32[4,8,2,16,128]{4,3,2,1,0:T(8,128)S(1)} copy-done((f32[4,8,2,16,128]{4,3,2,1,0:T(8,128)S(1)}, f32[4,8,2,16,128]{4,3,2,1,0:T(8,128)}, u32[]{:S(2)}) %copy-start.1) | copy-done | bytes 524312
  68.2 1.5 %shard_map.105 = (f32[64,4096]{1,0:T(8,128)}, f32[32,4096]{1,0:T(8,128)}) custom-call(f32[2,2,16,4096]{3,2,1,0:T(8,128)S(1)} %copy-done, f32[4,8,2,16,128]{4,3,2,1,0:T(8,128)S(1)} %copy-done.1), custom_call_target="tpu_custom_call" | custom-call | tf_op jit(solution)/shard_map/pallas_call | solution.py:549
Async XLA Ops:
  65.9 1.2 %copy-start = (f32[2,2,16,4096]{3,2,1,0:T(8,128)S(1)}, f32[2,2,16,4096]{3,2,1,0:T(8,128)}, u32[]{:S(2)}) copy-start(f32[2,2,16,4096]{3,2,1,0:T(8,128)} %get-tuple-element.4.mix_hbm) | copy-start | bytes 3145732
  67.1 1.0 %copy-start.1 = (f32[4,8,2,16,128]{4,3,2,1,0:T(8,128)S(1)}, f32[4,8,2,16,128]{4,3,2,1,0:T(8,128)}, u32[]{:S(2)}) copy-start(f32[4,8,2,16,128]{4,3,2,1,0:T(8,128)} %get-tuple-element.5.all_hbm) | copy-start | bytes 1572868

commit v4 on v3

--- a/solution.py
+++ b/solution.py
@@ -64,6 +64,18 @@
     @property
     def wide(self):
         return min(512, self.genes)
+
+
+CODES = 32767.0
+TINY = 1e-30
+
+
+def code(value, top):
+    return jnp.floor(value * (CODES / top) + 0.5).astype(jnp.int32).astype(jnp.int16)
+
+
+def decode(codes, top):
+    return codes.astype(jnp.int32).astype(F32) * (top * (1.0 / CODES))
 
 
 def pieces(value):
@@ -119,6 +131,7 @@
     noise_hbm,
     mix_out,
     all_out,
+    top_out,
     expr_ref,
     points_ref,
     weight_ref,
@@ -150,7 +163,9 @@
     mix_all,
     mix_sum,
     sum_ref,
+    row_ref,
     all_ref,
+    top_ref,
     load_sem,
     xy_sem,
     near_sem,
@@ -159,6 +174,7 @@
     lg_sem,
     mix_sem,
     all_sem,
+    all_keep,
     keep_sem,
 ):
     genes, lats, subs, blocks = plan.gene, plan.lat, plan.sub, plan.blocks
@@ -254,13 +270,14 @@
 
         lax.fori_loop(0, share, step, 0)
 
-    forward([(0, 0), (0, 1)], [])
+    forward([(0, 0)], [])
 
     pl.semaphore_wait(barrier, len(peers))
     copies = []
     for k, peer in enumerate(flat):
         copies.append(send(xy_ref.at[me], xy_ref.at[me], xy_sem, (k,), at(*peer)))
         copies[-1].start()
+    forward([(0, 1)], [])
     for load in loads[2:]:
         load.wait()
     gene_tiles = [slice(first, first + plan.wide) for first in range(0, plan.genes, plan.wide)]
@@ -413,10 +430,19 @@
         mix_keep(p).start()
 
     def gather_copies(j, h):
-        return [
-            send(all_ref.at[j, h], all_out.at[g, j, h], all_sem, (j, h, dg - 1), at(dg=dg))
-            for dg in range(1, genes)
-        ] + [pltpu.make_async_copy(all_ref.at[j, h], all_out.at[g, j, h], keep_sem.at[lats + 2 * j + h])]
+        out = []
+        for i, (src, dst) in enumerate(((all_ref, all_out), (top_ref, top_out))):
+            for dg in range(1, genes):
+                out.append(send(src.at[j, h], dst.at[g, j, h], all_sem, (i, j, h, dg - 1), at(dg=dg)))
+            out.append(pltpu.make_async_copy(src.at[j, h], dst.at[g, j, h], all_keep.at[i, j, h]))
+        return out
+
+    def gather(j, h):
+        value = row_ref[h]
+        top = jnp.maximum(jnp.max(jnp.abs(value), axis=0, keepdims=True), TINY)
+        top_ref[j, h] = top
+        all_ref[j, h] = code(value, top)
+        start(gather_copies(j, h))
 
     def backward(part, stages):
         def step(j, carry):
@@ -444,13 +470,13 @@
                         sum_ref[j, :, here] = sums[f]
                     else:
                         h, r = divmod(start_ // 128 + f, plan.points // 256)
-                        all_ref[j, h, r : r + 1, :] = jnp.sum(sum_ref[j, :, here] + sums[f], axis=0, keepdims=True)
+                        row_ref[h, r : r + 1, :] = jnp.sum(sum_ref[j, :, here] + sums[f], axis=0, keepdims=True)
                 if part == 1 and start_ + plan.tile == plan.points // 2:
-                    start(gather_copies(j, 0))
+                    gather(j, 0)
             if part == 1:
                 if plan.tile > plan.points // 2:
-                    start(gather_copies(j, 0))
-                start(gather_copies(j, 1))
+                    gather(j, 0)
+                gather(j, 1)
             return carry
 
         lax.fori_loop(0, share, step, 0)
@@ -475,8 +501,8 @@
         0,
         [
             (when(1), lambda: sum_near(1)),
-            (when(3), lambda: middle(1)),
-            (when(3), mix_part),
+            (when(4), lambda: middle(1)),
+            (when(4), mix_part),
             (when(6), lambda: sum_gene(1)),
             (when(6), mix_sub),
         ],
@@ -503,7 +529,7 @@
         mix_keep(p).wait()
 
 
-def lay_body(plan, mix_hbm, all_hbm, mix_out, ind_out, mix_ref, all_ref, ind_ref, in_sem, out_sem):
+def lay_body(plan, mix_hbm, all_hbm, top_hbm, mix_out, ind_out, mix_ref, all_ref, top_ref, row_ref, ind_ref, in_sem, out_sem):
     subs, lats, depth, _ = mix_hbm.shape
     parts = [(sub, p) for sub in range(subs) for p in range(lats)]
     mixes = [
@@ -513,21 +539,26 @@
         pltpu.make_async_copy(mix_ref.at[i], mix_out.at[pl.ds(i * depth, depth)], out_sem.at[i])
         for i in range(len(parts))
     ]
-    whole = pltpu.make_async_copy(all_hbm, all_ref, in_sem.at[len(parts)])
-    whole.start()
-    for copy in mixes:
+    wholes = [
+        pltpu.make_async_copy(all_hbm, all_ref, in_sem.at[len(parts)]),
+        pltpu.make_async_copy(top_hbm, top_ref, in_sem.at[len(parts) + 1]),
+    ]
+    for copy in wholes + mixes:
         copy.start()
-    whole.wait()
+    for copy in wholes:
+        copy.wait()
     last = []
     half = plan.points // 256
     for owner in range(plan.owners):
         base = owner * plan.share
         for slab in range(plan.split):
+            gene = owner * plan.split + slab
+            for j in range(plan.share):
+                for h in range(2):
+                    row_ref[gene, j, h * half : (h + 1) * half, :] = decode(all_ref[gene, j, h], top_ref[gene, j, h])
             for r in range(plan.points // 128):
                 first = slab * plan.points + r * 128
-                h, row = divmod(r, half)
-                piece = all_ref[owner * plan.split + slab, :, h, row, :]
-                ind_ref[base : base + plan.share, first : first + 128] = piece
+                ind_ref[base : base + plan.share, first : first + 128] = row_ref[gene, :, r, :]
         if plan.share % 8 == 0:
             rows = pl.ds(base, plan.share)
             last.append(pltpu.make_async_copy(ind_ref.at[rows], ind_out.at[rows], out_sem.at[len(parts) + owner]))
@@ -542,13 +573,13 @@
         copy.wait()
 
 
-def lay(plan, mix, all_):
+def lay(plan, mix, codes, tops):
     subs, lats, depth, genes = mix.shape
     parts = subs * lats
     anywhere = pl.BlockSpec(memory_space=pl.ANY)
     return pl.pallas_call(
         functools.partial(lay_body, plan),
-        in_specs=[anywhere] * 2,
+        in_specs=[anywhere] * 3,
         out_specs=[anywhere] * 2,
         out_shape=[
             jax.ShapeDtypeStruct((plan.total, genes), F32),
@@ -556,13 +587,15 @@
         ],
         scratch_shapes=[
             pltpu.VMEM((parts, depth, genes), F32),
-            pltpu.VMEM(all_.shape, F32),
+            pltpu.VMEM(codes.shape, jnp.int16),
+            pltpu.VMEM(tops.shape, F32),
+            pltpu.VMEM((plan.gene, plan.share, plan.points // 128, 128), F32),
             pltpu.VMEM((plan.lats, plan.count), F32),
-            pltpu.SemaphoreType.DMA((parts + 1,)),
+            pltpu.SemaphoreType.DMA((parts + 2,)),
             pltpu.SemaphoreType.DMA((parts + plan.owners,)),
         ],
-        compiler_params=pltpu.CompilerParams(vmem_limit_bytes=16 * 2**20),
-    )(mix, all_)
+        compiler_params=pltpu.CompilerParams(vmem_limit_bytes=60 * 2**20),
+    )(mix, codes, tops)
 
 
 def fused(plan, *args):
@@ -607,7 +640,9 @@
         pltpu.VMEM((lats, lats, depth, plan.genes), F32),
         pltpu.VMEM((lats, depth, plan.genes), F32),
         pltpu.VMEM((share, 8, plan.points), F32),
-        pltpu.VMEM((share, 2, plan.points // 256, 128), F32),
+        pltpu.VMEM((2, plan.points // 256, 128), F32),
+        pltpu.VMEM((share, 2, plan.points // 256, 128), jnp.int16),
+        pltpu.VMEM((share, 2, 1, 128), F32),
         dma((5,)),
         dma((2, max(1, flat))),
         dma((2, 2, max(1, subs - 1))),
@@ -615,16 +650,18 @@
         dma((2, 2, max(1, genes - 1))),
         dma((2, 2, max(1, flat))),
         dma((2, 3, max(1, subs - 1, lats - 1), lats)),
-        dma((2, share, 2, max(1, genes - 1))),
-        dma((lats + 2 * share,)),
+        dma((2, 2, share, 2, max(1, genes - 1))),
+        dma((2, share, 2)),
+        dma((lats,)),
     ]
     return pl.pallas_call(
         functools.partial(body, plan),
         in_specs=[vmem] * 4 + [anywhere] * 5,
-        out_specs=[anywhere, anywhere],
+        out_specs=[anywhere] * 3,
         out_shape=[
             jax.ShapeDtypeStruct((subs, lats, depth, plan.genes), F32),
-            jax.ShapeDtypeStruct((genes, share, 2, plan.points // 256, 128), F32),
+            jax.ShapeDtypeStruct((genes, share, 2, plan.points // 256, 128), jnp.int16),
+            jax.ShapeDtypeStruct((genes, share, 2, 1, 128), F32),
         ],
         scratch_shapes=scratch,
         compiler_params=pltpu.CompilerParams(
@@ -668,7 +705,7 @@
         first, cut = place // split * share, lax.rem(place, split) * plan.points
         inducing = lax.dynamic_slice(inducing, (0, first, cut), (2, share, plan.points))
         ind_weights = lax.dynamic_slice(ind_weights, (first, cut), (share, plan.points))
-    mix, gathered = fused(
+    mix, codes, tops = fused(
         plan,
         cell_index[None, :],
         coords_table,
@@ -680,7 +717,7 @@
         mixing,
         noise_prec[None, :],
     )
-    return lay(plan, mix, gathered)
+    return lay(plan, mix, codes, tops)
 
 
 def solution(mesh):

time: 70 us -> 69.8 us (level)
  local copies, waits for them, and re-layouts: 2.26 us -> 0 us
  Pallas kernels: 66.8 us -> 69 us
    unnamed x4 -> x0, local copies, waits for them, and re-layouts: 2.26 us -> none
    pallas_call x1, Pallas kernels: 65.3 us -> 66.6 us  [fused(): pl.pallas_call(functools.partial(body, plan), in_specs=[vmem] * 4 + [anyw...]
    pallas_call x1, Pallas kernels: 1.52 us -> 2.44 us  [lay(): pl.pallas_call(functools.partial(lay_body, plan), in_specs=[anywhere] * 3...]
where the time goes in v4:
time: 69.8 us; the launch traced here: 69.6 us
  Pallas kernels  69 us (99%)
    pallas_call x1, Pallas kernels, fused(): pl.pallas_call(functools.partial(body, plan), in_specs=[vmem] * 4 + [anyw...  66.6 us
    pallas_call x1, Pallas kernels, lay(): pl.pallas_call(functools.partial(lay_body, plan), in_specs=[anywhere] * 3...  2.44 us

profile of v4, /device:TPU:0, one launch (start us, length us, event | category | flops | bytes accessed | tf_op | source)
XLA Modules:
  0.0 69.6 jit_solution(2202649956852413724)
XLA Ops:
  0.6 66.6 %shard_map.104 = (f32[2,2,16,4096]{3,2,1,0:T(8,128)}, s16[4,8,2,16,128]{4,3,2,1,0:T(8,128)(2,1)}, f32[4,8,2,1,128]{4,3,2,1,0:T(1,128)}) custom-call(s32[1,256]{1,0:T(1,128)} %bitcast.5, f32[2,512]{1,0:T(2,128)} %coords_ref.1, f32[1,32]{1,0:T(1,128)} %bitcast.6, f32[1,32]{1,0:T(1,128)} %bitcast.7, bf16[512,4096]{1,0:T(8,128)(2,1)} %expr_hbm.1, ...), custom_call_target="tpu_custom_call" | custom-call | tf_op jit(solution)/shard_map/pallas_call | solution.py:657
  67.2 2.4 %shard_map.105 = (f32[64,4096]{1,0:T(8,128)}, f32[32,4096]{1,0:T(8,128)}) custom-call(f32[2,2,16,4096]{3,2,1,0:T(8,128)} %get-tuple-element.5.mix_hbm, s16[4,8,2,16,128]{4,3,2,1,0:T(8,128)(2,1)} %get-tuple-element.6.all_hbm, f32[4,8,2,1,128]{4,3,2,1,0:T(1,128)} %get-tuple-element.7.top_hbm), custom_call_target="tpu_custom_call" | custom-call | tf_op jit(solution)/shard_map/pallas_call | solution.py:580

commit v5 on v3

--- a/solution.py
+++ b/solution.py
@@ -15,6 +15,7 @@
 SPARE = 21
 CENTER = 0.5
 LOG2E = math.log2(math.e)
+CACHE = 40 * 2**20
 LEFT = (0, 0, 1, 1, 0, 2)
 RIGHT = (0, 1, 0, 1, 2, 0)
 
@@ -62,8 +63,42 @@
         return min(256, self.points)
 
     @property
+    def cached(self):
+        return min(self.points // self.tile, CACHE // (self.share * self.blocks * self.half * self.tile * 4))
+
+    @property
     def wide(self):
         return min(512, self.genes)
+
+
+BIAS = 128
+LEAST = 2.0**-120
+
+
+def bit_rows(shape):
+    row = lax.broadcasted_iota(jnp.int32, shape, 0)
+    return row, row < 8
+
+
+def code(value):
+    top = jnp.maximum(jnp.max(jnp.abs(value), axis=0, keepdims=True), LEAST)
+    power = jnp.floor(jnp.log(top) * LOG2E + 1e-5) + 1.0
+    row, marked = bit_rows(value.shape)
+    scaled = value * jnp.exp2(15.0 - power)
+    fine = jnp.clip(jnp.floor(scaled + 0.5), -32767.0, 32767.0).astype(jnp.int32)
+    coarse = jnp.clip(jnp.floor(scaled * 0.5 + 0.5), -16383.0, 16383.0).astype(jnp.int32) * 2
+    place = jnp.where(marked, row, 0)
+    bit = jnp.bitwise_and(jnp.right_shift(power.astype(jnp.int32) + BIAS, place), 1)
+    return jnp.where(marked, coarse + bit, fine).astype(jnp.int16)
+
+
+def decode(codes):
+    codes = codes.astype(jnp.int32)
+    row, marked = bit_rows(codes.shape)
+    bit = jnp.where(marked, jnp.bitwise_and(codes, 1), 0)
+    weight = jnp.left_shift(bit, jnp.where(marked, row, 0)).astype(F32)
+    power = jnp.sum(weight, axis=0, keepdims=True) - float(BIAS)
+    return (codes - bit).astype(F32) * jnp.exp2(power - 15.0)
 
 
 def pieces(value):
@@ -150,7 +185,9 @@
     mix_all,
     mix_sum,
     sum_ref,
+    row_ref,
     all_ref,
+    cache_ref,
     load_sem,
     xy_sem,
     near_sem,
@@ -159,6 +196,7 @@
     lg_sem,
     mix_sem,
     all_sem,
+    all_keep,
     keep_sem,
 ):
     genes, lats, subs, blocks = plan.gene, plan.lat, plan.sub, plan.blocks
@@ -227,10 +265,13 @@
         return lax.rem(me + k, blocks)
 
     def flush(part):
+        lane = lax.broadcasted_iota(jnp.int32, (half, 128), 1)
         for k in range(blocks):
+            sums = jnp.zeros((half, 128), F32)
             for j in range(share):
-                row = jnp.sum(total_ref[j, 2 * k + part].T, axis=0, keepdims=True)
-                part_ref[part, lax.rem(ring(k), subs), ring(k) // subs, j : j + 1, :] = row
+                column = jnp.sum(total_ref[j, 2 * k + part], axis=1, keepdims=True)
+                sums = jnp.where(lane == j, column, sums)
+            part_ref[part, lax.rem(ring(k), subs), ring(k) // subs] = sums.T[:share, :]
         start(near_copies(part))
 
     def forward(units, stages):
@@ -246,6 +287,8 @@
                     value = jnp.exp2(
                         jnp.dot(feat, table_ref[j, :, cols].astype(BF16), preferred_element_type=F32)
                     )
+                    if part == 1 and start // plan.tile < plan.cached:
+                        cache_ref[j, k, start // plan.tile] = value
                     for first in range(0, plan.tile, 128):
                         w = table_ref[j, SPARE : SPARE + 1, start + first : start + first + 128]
                         total = total + value[:, first : first + 128] * w
@@ -254,13 +297,14 @@
 
         lax.fori_loop(0, share, step, 0)
 
-    forward([(0, 0), (0, 1)], [])
+    forward([(0, 0)], [])
 
     pl.semaphore_wait(barrier, len(peers))
     copies = []
     for k, peer in enumerate(flat):
         copies.append(send(xy_ref.at[me], xy_ref.at[me], xy_sem, (k,), at(*peer)))
         copies[-1].start()
+    forward([(0, 1)], [])
     for load in loads[2:]:
         load.wait()
     gene_tiles = [slice(first, first + plan.wide) for first in range(0, plan.genes, plan.wide)]
@@ -400,23 +444,22 @@
             value = mix_ref[s, p]
             for ds in range(1, subs):
                 value = value + mix_near[ds - 1, p]
-            mix_all[l, p] = value
+            mix_all[l, p] = code(value)
             start(mix_lat_copies(p))
 
     def mix_lat(p):
         wait(mix_lat_copies(p))
-        value = mix_all[0, p]
+        value = decode(mix_all[0, p])
         for lat in range(1, lats):
-            value = value + mix_all[lat, p]
+            value = value + decode(mix_all[lat, p])
         mix_sum[p] = value
         start(mix_back_copies(p))
         mix_keep(p).start()
 
-    def gather_copies(j, h):
+    def gather_copies(j):
         return [
-            send(all_ref.at[j, h], all_out.at[g, j, h], all_sem, (j, h, dg - 1), at(dg=dg))
-            for dg in range(1, genes)
-        ] + [pltpu.make_async_copy(all_ref.at[j, h], all_out.at[g, j, h], keep_sem.at[lats + 2 * j + h])]
+            send(all_ref.at[j], all_out.at[g, j], all_sem, (j, dg - 1), at(dg=dg)) for dg in range(1, genes)
+        ] + [pltpu.make_async_copy(all_ref.at[j], all_out.at[g, j], all_keep.at[j])]
 
     def backward(part, stages):
         def step(j, carry):
@@ -424,33 +467,57 @@
                 pl.when(j == when)(stage)
             row = lax.broadcasted_iota(jnp.int32, (plan.turned, 128), 0)
             select = (lax.rem(row, share) == j).astype(F32).astype(BF16)
-            for block in range(blocks):
-                turned = lgt_ref[block * half : (block + 1) * half, :]
-                wide_ref[block] = jnp.dot(turned, select, preferred_element_type=F32)
-            for start_ in range(0, plan.points, plan.tile):
-                cols = slice(start_, start_ + plan.tile)
-                points = table_ref[j, :, cols].astype(BF16)
-                sums = [None] * (plan.tile // 128)
-                for block in range(blocks):
-                    feat = feat_ref[block * rows + part * half : block * rows + (part + 1) * half, :]
-                    value = jnp.exp2(jnp.dot(feat, points, preferred_element_type=F32))
-                    for f in range(plan.tile // 128):
-                        term = value[:, f * 128 : (f + 1) * 128] * wide_ref[block]
+            for k in range(blocks):
+                place = pl.multiple_of(ring(k) * half, half)
+                turned = lgt_ref[pl.ds(place, half), :]
+                wide_ref[k] = jnp.dot(turned, select, preferred_element_type=F32)
+            tiles = list(range(plan.points // plan.tile))
+            kept = tiles[: plan.cached] if part == 1 else []
+            fresh = tiles[len(kept) :]
+            lanes = plan.tile // 128
+            held = [(t, f) for t in kept for f in range(lanes)]
+            held_sums = [None] * len(held)
+            groups = [(k, r) for k in range(blocks) for r in range(0, half, 8)] if held else []
+            steps = len(fresh) * blocks
+            pace = -(-len(groups) // max(1, steps))
+
+            def settle(sums, t, f):
+                r = t * lanes + f
+                here = slice(r * 128, (r + 1) * 128)
+                if part == 0:
+                    sum_ref[j, :, here] = sums
+                else:
+                    row_ref[r : r + 1, :] = jnp.sum(sum_ref[j, :, here] + sums, axis=0, keepdims=True)
+
+            def spend(groups):
+                for k, r in groups:
+                    wide = wide_ref[k, r : r + 8, :]
+                    for i, (t, f) in enumerate(held):
+                        term = cache_ref[j, k, t, r : r + 8, f * 128 : (f + 1) * 128] * wide
+                        held_sums[i] = term if held_sums[i] is None else held_sums[i] + term
+
+            for t in fresh:
+                points = table_ref[j, :, t * plan.tile : (t + 1) * plan.tile].astype(BF16)
+                sums = [None] * lanes
+                for k in range(blocks):
+                    place = pl.multiple_of(ring(k) * rows + part * half, half)
+                    value = jnp.exp2(
+                        jnp.dot(feat_ref[pl.ds(place, half), :], points, preferred_element_type=F32)
+                    )
+                    for f in range(lanes):
+                        term = value[:, f * 128 : (f + 1) * 128] * wide_ref[k]
                         term = jnp.sum(term.reshape(half // 8, 8, 128), axis=0)
                         sums[f] = term if sums[f] is None else sums[f] + term
-                for f in range(plan.tile // 128):
-                    here = slice(start_ + f * 128, start_ + (f + 1) * 128)
-                    if part == 0:
-                        sum_ref[j, :, here] = sums[f]
-                    else:
-                        h, r = divmod(start_ // 128 + f, plan.points // 256)
-                        all_ref[j, h, r : r + 1, :] = jnp.sum(sum_ref[j, :, here] + sums[f], axis=0, keepdims=True)
-                if part == 1 and start_ + plan.tile == plan.points // 2:
-                    start(gather_copies(j, 0))
+                    spend(groups[:pace])
+                    groups = groups[pace:]
+                for f in range(lanes):
+                    settle(sums[f], t, f)
+            spend(groups)
+            for (t, f), sums in zip(held, held_sums):
+                settle(sums, t, f)
             if part == 1:
-                if plan.tile > plan.points // 2:
-                    start(gather_copies(j, 0))
-                start(gather_copies(j, 1))
+                all_ref[j] = code(row_ref[...])
+                start(gather_copies(j))
             return carry
 
         lax.fori_loop(0, share, step, 0)
@@ -475,8 +542,8 @@
         0,
         [
             (when(1), lambda: sum_near(1)),
-            (when(3), lambda: middle(1)),
-            (when(3), mix_part),
+            (when(4), lambda: middle(1)),
+            (when(4), mix_part),
             (when(6), lambda: sum_gene(1)),
             (when(6), mix_sub),
         ],
@@ -488,13 +555,12 @@
         for p in range(early):
             mix_lat(p)
 
-    backward(1, [(when(5), first_parts)])
+    backward(1, [(when(6), first_parts)])
     for p in range(early, lats):
         mix_lat(p)
 
     def finish(j, carry):
-        wait(gather_copies(j, 0))
-        wait(gather_copies(j, 1))
+        wait(gather_copies(j))
         return carry
 
     lax.fori_loop(0, share, finish, 0)
@@ -503,7 +569,7 @@
         mix_keep(p).wait()
 
 
-def lay_body(plan, mix_hbm, all_hbm, mix_out, ind_out, mix_ref, all_ref, ind_ref, in_sem, out_sem):
+def lay_body(plan, mix_hbm, all_hbm, mix_out, ind_out, mix_ref, all_ref, row_ref, ind_ref, in_sem, out_sem):
     subs, lats, depth, _ = mix_hbm.shape
     parts = [(sub, p) for sub in range(subs) for p in range(lats)]
     mixes = [
@@ -514,20 +580,19 @@
         for i in range(len(parts))
     ]
     whole = pltpu.make_async_copy(all_hbm, all_ref, in_sem.at[len(parts)])
-    whole.start()
-    for copy in mixes:
+    for copy in [whole] + mixes:
         copy.start()
     whole.wait()
     last = []
-    half = plan.points // 256
     for owner in range(plan.owners):
         base = owner * plan.share
         for slab in range(plan.split):
+            gene = owner * plan.split + slab
+            for j in range(plan.share):
+                row_ref[gene, j] = decode(all_ref[gene, j])
             for r in range(plan.points // 128):
                 first = slab * plan.points + r * 128
-                h, row = divmod(r, half)
-                piece = all_ref[owner * plan.split + slab, :, h, row, :]
-                ind_ref[base : base + plan.share, first : first + 128] = piece
+                ind_ref[base : base + plan.share, first : first + 128] = row_ref[gene, :, r, :]
         if plan.share % 8 == 0:
             rows = pl.ds(base, plan.share)
             last.append(pltpu.make_async_copy(ind_ref.at[rows], ind_out.at[rows], out_sem.at[len(parts) + owner]))
@@ -542,7 +607,7 @@
         copy.wait()
 
 
-def lay(plan, mix, all_):
+def lay(plan, mix, codes):
     subs, lats, depth, genes = mix.shape
     parts = subs * lats
     anywhere = pl.BlockSpec(memory_space=pl.ANY)
@@ -556,13 +621,14 @@
         ],
         scratch_shapes=[
             pltpu.VMEM((parts, depth, genes), F32),
-            pltpu.VMEM(all_.shape, F32),
+            pltpu.VMEM(codes.shape, jnp.int16),
+            pltpu.VMEM((plan.gene, plan.share, plan.points // 128, 128), F32),
             pltpu.VMEM((plan.lats, plan.count), F32),
             pltpu.SemaphoreType.DMA((parts + 1,)),
             pltpu.SemaphoreType.DMA((parts + plan.owners,)),
         ],
-        compiler_params=pltpu.CompilerParams(vmem_limit_bytes=16 * 2**20),
-    )(mix, all_)
+        compiler_params=pltpu.CompilerParams(vmem_limit_bytes=60 * 2**20),
+    )(mix, codes)
 
 
 def fused(plan, *args):
@@ -604,10 +670,12 @@
         pltpu.VMEM((blocks, half, 128), F32),
         pltpu.VMEM((subs, lats, depth, plan.genes), F32),
         pltpu.VMEM((max(1, subs - 1), lats, depth, plan.genes), F32),
-        pltpu.VMEM((lats, lats, depth, plan.genes), F32),
+        pltpu.VMEM((lats, lats, depth, plan.genes), jnp.int16),
         pltpu.VMEM((lats, depth, plan.genes), F32),
         pltpu.VMEM((share, 8, plan.points), F32),
-        pltpu.VMEM((share, 2, plan.points // 256, 128), F32),
+        pltpu.VMEM((plan.points // 128, 128), F32),
+        pltpu.VMEM((share, plan.points // 128, 128), jnp.int16),
+        pltpu.VMEM((share, blocks, max(1, plan.cached), half, plan.tile), F32),
         dma((5,)),
         dma((2, max(1, flat))),
         dma((2, 2, max(1, subs - 1))),
@@ -615,20 +683,21 @@
         dma((2, 2, max(1, genes - 1))),
         dma((2, 2, max(1, flat))),
         dma((2, 3, max(1, subs - 1, lats - 1), lats)),
-        dma((2, share, 2, max(1, genes - 1))),
-        dma((lats + 2 * share,)),
+        dma((2, share, max(1, genes - 1))),
+        dma((share,)),
+        dma((lats,)),
     ]
     return pl.pallas_call(
         functools.partial(body, plan),
         in_specs=[vmem] * 4 + [anywhere] * 5,
-        out_specs=[anywhere, anywhere],
+        out_specs=[anywhere] * 2,
         out_shape=[
             jax.ShapeDtypeStruct((subs, lats, depth, plan.genes), F32),
-            jax.ShapeDtypeStruct((genes, share, 2, plan.points // 256, 128), F32),
+            jax.ShapeDtypeStruct((genes, share, plan.points // 128, 128), jnp.int16),
         ],
         scratch_shapes=scratch,
         compiler_params=pltpu.CompilerParams(
-            collective_id=0, has_side_effects=True, vmem_limit_bytes=60 * 2**20
+            collective_id=0, has_side_effects=True, vmem_limit_bytes=67043328
         ),
     )(*args)
 
@@ -668,7 +737,7 @@
         first, cut = place // split * share, lax.rem(place, split) * plan.points
         inducing = lax.dynamic_slice(inducing, (0, first, cut), (2, share, plan.points))
         ind_weights = lax.dynamic_slice(ind_weights, (first, cut), (share, plan.points))
-    mix, gathered = fused(
+    mix, codes = fused(
         plan,
         cell_index[None, :],
         coords_table,
@@ -680,7 +749,7 @@
         mixing,
         noise_prec[None, :],
     )
-    return lay(plan, mix, gathered)
+    return lay(plan, mix, codes)
 
 
 def solution(mesh):

time: 70 us -> 64.5 us (0.921)
  Pallas kernels: 66.8 us -> 63.7 us
  local copies, waits for them, and re-layouts: 2.26 us -> 0 us
    pallas_call x1, Pallas kernels: 65.3 us -> 61.2 us  [fused(): pl.pallas_call(functools.partial(body, plan), in_specs=[vmem] * 4 + [anyw...]
    unnamed x4 -> x0, local copies, waits for them, and re-layouts: 2.26 us -> none
    pallas_call x1, Pallas kernels: 1.52 us -> 2.47 us  [lay(): pl.pallas_call(functools.partial(lay_body, plan), in_specs=[anywhere] * 2...]
where the time goes in v5:
time: 64.5 us; the launch traced here: 64.3 us
  Pallas kernels  63.7 us (99%)
    pallas_call x1, Pallas kernels, fused(): pl.pallas_call(functools.partial(body, plan), in_specs=[vmem] * 4 + [anyw...  61.2 us
    pallas_call x1, Pallas kernels, lay(): pl.pallas_call(functools.partial(lay_body, plan), in_specs=[anywhere] * 2...  2.47 us

profile of v5, /device:TPU:0, one launch (start us, length us, event | category | flops | bytes accessed | tf_op | source)
XLA Modules:
  0.0 64.3 jit_solution(12975423492767824693)
XLA Ops:
  0.6 61.2 %shard_map.104 = (f32[2,2,16,4096]{3,2,1,0:T(8,128)}, s16[4,8,32,128]{3,2,1,0:T(8,128)(2,1)}) custom-call(s32[1,256]{1,0:T(1,128)} %bitcast.5, f32[2,512]{1,0:T(2,128)} %coords_ref.1, f32[1,32]{1,0:T(1,128)} %bitcast.6, f32[1,32]{1,0:T(1,128)} %bitcast.7, bf16[512,4096]{1,0:T(8,128)(2,1)} %expr_hbm.1, f32[2,32,4096]{2,1,0:T(8,128)} %points_hbm.1, ...), custom_call_target="tpu_custom_call" | custom-call | tf_op jit(solution)/shard_map/pallas_call | solution.py:690
  61.8 2.5 %shard_map.105 = (f32[64,4096]{1,0:T(8,128)}, f32[32,4096]{1,0:T(8,128)}) custom-call(f32[2,2,16,4096]{3,2,1,0:T(8,128)} %get-tuple-element.4.mix_hbm, s16[4,8,32,128]{3,2,1,0:T(8,128)(2,1)} %get-tuple-element.5.all_hbm), custom_call_target="tpu_custom_call" | custom-call | tf_op jit(solution)/shard_map/pallas_call | solution.py:614

commit v6 on v5

--- a/solution.py
+++ b/solution.py
@@ -15,6 +15,7 @@
 SPARE = 21
 CENTER = 0.5
 LOG2E = math.log2(math.e)
+PACK = 20
 CACHE = 40 * 2**20
 LEFT = (0, 0, 1, 1, 0, 2)
 RIGHT = (0, 1, 0, 1, 2, 0)
@@ -143,10 +144,10 @@
 
 def body(
     plan,
-    index_ref,
-    coords_ref,
-    length_ref,
-    height_ref,
+    index_hbm,
+    coords_hbm,
+    length_hbm,
+    height_hbm,
     expr_hbm,
     points_hbm,
     weight_hbm,
@@ -154,6 +155,10 @@
     noise_hbm,
     mix_out,
     all_out,
+    index_ref,
+    coords_ref,
+    length_ref,
+    height_ref,
     expr_ref,
     points_ref,
     weight_ref,
@@ -231,7 +236,13 @@
         pltpu.make_async_copy(mixing_hbm, mixing_ref, load_sem.at[3]),
         pltpu.make_async_copy(noise_hbm, noise_ref, load_sem.at[4]),
     ]
-    for load in loads[:2]:
+    small = [
+        pltpu.make_async_copy(index_hbm, index_ref, load_sem.at[5]),
+        pltpu.make_async_copy(coords_hbm, coords_ref, load_sem.at[6]),
+        pltpu.make_async_copy(length_hbm, length_ref, load_sem.at[7]),
+        pltpu.make_async_copy(height_hbm, height_ref, load_sem.at[8]),
+    ]
+    for load in small + loads[:2]:
         load.start()
 
     far = [(dg, dl, 0) for dg in range(genes) for dl in range(lats) if dg or dl]
@@ -241,6 +252,8 @@
     for peer in peers:
         pl.semaphore_signal(barrier, inc=1, device_id=at(*peer), device_id_type=pl.DeviceIdType.MESH)
 
+    for load in small:
+        load.wait()
     pick = lax.broadcasted_iota(jnp.int32, (plan.table, rows), 0) == index_ref[...]
     pick_ref[...] = pick.astype(F32).astype(BF16)
     local = jnp.zeros((2, rows), F32)
@@ -274,37 +287,43 @@
             part_ref[part, lax.rem(ring(k), subs), ring(k) // subs] = sums.T[:share, :]
         start(near_copies(part))
 
-    def forward(units, stages):
-        def step(j, carry):
+    def forward(units, stages=(), low=0, high=share, step=1):
+        step = math.gcd(step, high - low) if high > low else 1
+
+        def products(i, carry):
             for when, stage in stages:
-                pl.when(j == when)(stage)
-            for k, part in units:
-                place = pl.multiple_of(ring(k) * rows + part * half, half)
-                feat = feat_ref[pl.ds(place, half), :]
-                total = jnp.zeros((half, 128), F32)
-                for start in range(0, plan.points, plan.tile):
-                    cols = slice(start, start + plan.tile)
-                    value = jnp.exp2(
-                        jnp.dot(feat, table_ref[j, :, cols].astype(BF16), preferred_element_type=F32)
-                    )
-                    if part == 1 and start // plan.tile < plan.cached:
-                        cache_ref[j, k, start // plan.tile] = value
-                    for first in range(0, plan.tile, 128):
-                        w = table_ref[j, SPARE : SPARE + 1, start + first : start + first + 128]
-                        total = total + value[:, first : first + 128] * w
-                total_ref[j, 2 * k + part] = total
+                pl.when(i == (when - low) // step)(stage)
+            for j in [low + i * step + d for d in range(step)]:
+                for k, part in units:
+                    place = pl.multiple_of(ring(k) * rows + part * half, half)
+                    feat = feat_ref[pl.ds(place, half), :]
+                    total = jnp.zeros((half, 128), F32)
+                    for start in range(0, plan.points, plan.tile):
+                        cols = slice(start, start + plan.tile)
+                        value = jnp.exp2(
+                            jnp.dot(feat, table_ref[j, :, cols].astype(BF16), preferred_element_type=F32)
+                        )
+                        if part == 1 and start // plan.tile < plan.cached:
+                            cache_ref[j, k, start // plan.tile] = value
+                        for first in range(0, plan.tile, 128):
+                            w = table_ref[j, SPARE : SPARE + 1, start + first : start + first + 128]
+                            total = total + value[:, first : first + 128] * w
+                    total_ref[j, 2 * k + part] = total
             return carry
 
-        lax.fori_loop(0, share, step, 0)
-
-    forward([(0, 0)], [])
+        lax.fori_loop(0, (high - low) // step, products, 0)
+
+    def when(k):
+        return k * share // 8
+
+    forward([(0, 0)], step=4)
 
     pl.semaphore_wait(barrier, len(peers))
     copies = []
     for k, peer in enumerate(flat):
         copies.append(send(xy_ref.at[me], xy_ref.at[me], xy_sem, (k,), at(*peer)))
         copies[-1].start()
-    forward([(0, 1)], [])
+    forward([(0, 1)], high=when(4), step=4)
     for load in loads[2:]:
         load.wait()
     gene_tiles = [slice(first, first + plan.wide) for first in range(0, plan.genes, plan.wide)]
@@ -477,7 +496,8 @@
             lanes = plan.tile // 128
             held = [(t, f) for t in kept for f in range(lanes)]
             held_sums = [None] * len(held)
-            groups = [(k, r) for k in range(blocks) for r in range(0, half, 8)] if held else []
+            packs = [range(i, min(i + PACK, len(held))) for i in range(0, len(held), PACK)]
+            groups = [(pack, k, r) for pack in packs for k in range(blocks) for r in range(0, half, 8)]
             steps = len(fresh) * blocks
             pace = -(-len(groups) // max(1, steps))
 
@@ -490,9 +510,10 @@
                     row_ref[r : r + 1, :] = jnp.sum(sum_ref[j, :, here] + sums, axis=0, keepdims=True)
 
             def spend(groups):
-                for k, r in groups:
+                for pack, k, r in groups:
                     wide = wide_ref[k, r : r + 8, :]
-                    for i, (t, f) in enumerate(held):
+                    for i in pack:
+                        t, f = held[i]
                         term = cache_ref[j, k, t, r : r + 8, f * 128 : (f + 1) * 128] * wide
                         held_sums[i] = term if held_sums[i] is None else held_sums[i] + term
 
@@ -522,18 +543,14 @@
 
         lax.fori_loop(0, share, step, 0)
 
-    def when(k):
-        return k * share // 8
-
-    forward([(k, 0) for k in range(1, blocks)], [])
+    forward([(k, 0) for k in range(1, blocks)], step=2)
     flush(0)
+    forward([(0, 1)], low=when(4), high=when(6), step=2)
+    sum_near(0)
+    forward([(0, 1)], low=when(6), step=2)
     forward(
         [(k, 1) for k in range(1, blocks)],
-        [
-            (when(1), lambda: sum_near(0)),
-            (when(5), lambda: middle(0)),
-            (when(7), lambda: sum_gene(0)),
-        ],
+        [(when(3), lambda: middle(0)), (when(7), lambda: sum_gene(0))],
     )
     flush(1)
     lgside_ref[...] = jnp.zeros_like(lgside_ref)
@@ -541,11 +558,11 @@
     backward(
         0,
         [
-            (when(1), lambda: sum_near(1)),
-            (when(4), lambda: middle(1)),
-            (when(4), mix_part),
-            (when(6), lambda: sum_gene(1)),
-            (when(6), mix_sub),
+            (when(0), lambda: sum_near(1)),
+            (when(3), lambda: middle(1)),
+            (when(3), mix_part),
+            (when(5), lambda: sum_gene(1)),
+            (when(5), mix_sub),
         ],
     )
     turn(1)
@@ -639,9 +656,12 @@
     dma = pltpu.SemaphoreType.DMA
     far = genes * lats - 1
     flat = blocks - 1
-    vmem = pl.BlockSpec(memory_space=pltpu.VMEM)
     anywhere = pl.BlockSpec(memory_space=pl.ANY)
     scratch = [
+        pltpu.VMEM((1, rows), jnp.int32),
+        pltpu.VMEM((2, plan.table), F32),
+        pltpu.VMEM((1, plan.lats), F32),
+        pltpu.VMEM((1, plan.lats), F32),
         pltpu.VMEM((plan.table, plan.genes), BF16),
         pltpu.VMEM((2, share, plan.points), F32),
         pltpu.VMEM((share, plan.points), F32),
@@ -676,7 +696,7 @@
         pltpu.VMEM((plan.points // 128, 128), F32),
         pltpu.VMEM((share, plan.points // 128, 128), jnp.int16),
         pltpu.VMEM((share, blocks, max(1, plan.cached), half, plan.tile), F32),
-        dma((5,)),
+        dma((9,)),
         dma((2, max(1, flat))),
         dma((2, 2, max(1, subs - 1))),
         dma((2, 2, max(1, far))),
@@ -689,7 +709,7 @@
     ]
     return pl.pallas_call(
         functools.partial(body, plan),
-        in_specs=[vmem] * 4 + [anywhere] * 5,
+        in_specs=[anywhere] * 9,
         out_specs=[anywhere] * 2,
         out_shape=[
             jax.ShapeDtypeStruct((subs, lats, depth, plan.genes), F32),

time: 64.5 us -> 60.8 us (0.943)
  Pallas kernels: 63.7 us -> 59.9 us
    pallas_call x1, Pallas kernels: 61.2 us -> 57.4 us  [fused(): pl.pallas_call(functools.partial(body, plan), in_specs=[anywhere] * 9, ou...]
where the time goes in v6:
time: 60.8 us; the launch traced here: 60.7 us
  Pallas kernels  59.9 us (99%)
  between operations  0.8 us (1%)
    pallas_call x1, Pallas kernels, fused(): pl.pallas_call(functools.partial(body, plan), in_specs=[anywhere] * 9, ou...  57.4 us
    pallas_call x1, Pallas kernels, lay(): pl.pallas_call(functools.partial(lay_body, plan), in_specs=[anywhere] * 2...  2.47 us

profile of v6, /device:TPU:0, one launch (start us, length us, event | category | flops | bytes accessed | tf_op | source)
XLA Modules:
  0.0 60.7 jit_solution(11677819562200888895)
XLA Ops:
  0.6 57.4 %shard_map.104 = (f32[2,2,16,4096]{3,2,1,0:T(8,128)}, s16[4,8,32,128]{3,2,1,0:T(8,128)(2,1)}) custom-call(s32[1,256]{1,0:T(1,128)} %bitcast.5, f32[2,512]{1,0:T(2,128)} %coords_hbm.1, f32[1,32]{1,0:T(1,128)} %bitcast.6, f32[1,32]{1,0:T(1,128)} %bitcast.7, bf16[512,4096]{1,0:T(8,128)(2,1)} %expr_hbm.1, f32[2,32,4096]{2,1,0:T(8,128)} %points_hbm.1, ...), custom_call_target="tpu_custom_call" | custom-call | tf_op jit(solution)/shard_map/pallas_call | solution.py:710
  58.0 2.5 %shard_map.105 = (f32[64,4096]{1,0:T(8,128)}, f32[32,4096]{1,0:T(8,128)}) custom-call(f32[2,2,16,4096]{3,2,1,0:T(8,128)} %get-tuple-element.4.mix_hbm, s16[4,8,32,128]{3,2,1,0:T(8,128)(2,1)} %get-tuple-element.5.all_hbm), custom_call_target="tpu_custom_call" | custom-call | tf_op jit(solution)/shard_map/pallas_call | solution.py:631

commit v7 on v6

--- a/solution.py
+++ b/solution.py
@@ -193,6 +193,7 @@
     row_ref,
     all_ref,
     cache_ref,
+    far_ref,
     load_sem,
     xy_sem,
     near_sem,
@@ -201,7 +202,6 @@
     lg_sem,
     mix_sem,
     all_sem,
-    all_keep,
     keep_sem,
 ):
     genes, lats, subs, blocks = plan.gene, plan.lat, plan.sub, plan.blocks
@@ -222,6 +222,11 @@
             device_id=device,
             device_id_type=pl.DeviceIdType.MESH,
         )
+
+    def drain(sems, k, sent, got):
+        if sent is not None:
+            pltpu.make_async_copy(sent, sent, sems.at[(0, *k)]).wait()
+        pltpu.make_async_copy(got, got, sems.at[(1, *k)]).wait()
 
     if plan.sliced:
         points_src, weight_src = points_hbm, weight_hbm
@@ -319,10 +324,8 @@
     forward([(0, 0)], step=4)
 
     pl.semaphore_wait(barrier, len(peers))
-    copies = []
-    for k, peer in enumerate(flat):
-        copies.append(send(xy_ref.at[me], xy_ref.at[me], xy_sem, (k,), at(*peer)))
-        copies[-1].start()
+    for peer in flat:
+        send(xy_ref.at[me], xy_ref.at[me], xy_sem, (), at(*peer)).start()
     forward([(0, 1)], high=when(4), step=4)
     for load in loads[2:]:
         load.wait()
@@ -332,8 +335,9 @@
             pick_ref[...], expr_ref[:, cols], (((0,), (0,)), ((), ())), preferred_element_type=F32
         )
         seen_ref[:, cols] = seen.astype(BF16)
-    for copy in copies:
-        copy.wait()
+    if flat:
+        others = xy_ref.at[pl.ds(0, blocks - 1)]
+        drain(xy_sem, (), others, others)
     for k in range(1, blocks):
         cell_features(plan, ring(k), xy_ref, side_ref, feat_ref)
 
@@ -345,10 +349,10 @@
 
     def latent_copies(part):
         out = []
-        for k, peer in enumerate(far):
+        for peer in far:
             target = at(*peer)
             out.append(
-                send(final_ref.at[part, target["lat"]], latent_recv.at[part, g, l], latent_sem, (part, k), target)
+                send(final_ref.at[part, target["lat"]], latent_recv.at[part, g, l], latent_sem, (part,), target)
             )
         return out
 
@@ -357,14 +361,14 @@
         for dg in range(1, genes):
             target = at(dg=dg)
             source = chunk_ref.at[part, target["gene"] // plan.split]
-            out.append(send(source, rs_ref.at[part, dg - 1], rs_sem, (part, dg - 1), target))
+            out.append(send(source, rs_ref.at[part, dg - 1], rs_sem, (part,), target))
         return out
 
     def lg_copies(part):
         out = []
-        for k, peer in enumerate(flat):
+        for peer in flat:
             target = at(*peer)
-            out.append(send(own_ref.at[part, target["lat"]], lg_ref.at[part, me], lg_sem, (part, k), target))
+            out.append(send(own_ref.at[part, target["lat"]], lg_ref.at[part, me], lg_sem, (part,), target))
         return out
 
     def start(copies):
@@ -383,10 +387,10 @@
         value = value * height[None]
         final_ref[part] = value.astype(final_ref.dtype)
         start(latent_copies(part))
-        latent_recv[part, g, l] = final_ref[part, l]
+        pltpu.make_async_copy(final_ref.at[part, l], latent_recv.at[part, g, l], latent_sem.at[1, part]).start()
 
     def middle(part):
-        wait(latent_copies(part))
+        drain(latent_sem, (part,), far_ref if far else None, latent_recv.at[part])
         for lat in range(lats):
             for own in range(plan.owners):
                 first = own * plan.split
@@ -415,16 +419,17 @@
         start(rs_copies(part))
 
     def sum_gene(part):
-        wait(rs_copies(part))
+        if genes > 1:
+            drain(rs_sem, (part,), rs_ref.at[part], rs_ref.at[part])
         value = chunk_ref[part, owner]
         for dg in range(1, genes):
             value = value + rs_ref[part, dg - 1]
         own_ref[part] = value
         start(lg_copies(part))
-        lg_ref[part, me] = own_ref[part, l]
+        pltpu.make_async_copy(own_ref.at[part, l], lg_ref.at[part, me], lg_sem.at[1, part]).start()
 
     def turn(part):
-        wait(lg_copies(part))
+        drain(lg_sem, (part,), lg_ref.at[part, pl.ds(0, blocks - 1)] if flat else None, lg_ref.at[part])
         for block in range(blocks):
             for p, piece in enumerate(pieces(lg_ref[part, block] * height)):
                 lgside_ref[p * share : (p + 1) * share, :] = piece
@@ -477,8 +482,8 @@
 
     def gather_copies(j):
         return [
-            send(all_ref.at[j], all_out.at[g, j], all_sem, (j, dg - 1), at(dg=dg)) for dg in range(1, genes)
-        ] + [pltpu.make_async_copy(all_ref.at[j], all_out.at[g, j], all_keep.at[j])]
+            send(all_ref.at[j], all_out.at[g, j], all_sem, (), at(dg=dg)) for dg in range(1, genes)
+        ] + [pltpu.make_async_copy(all_ref.at[j], all_out.at[g, j], all_sem.at[1])]
 
     def backward(part, stages):
         def step(j, carry):
@@ -576,31 +581,19 @@
     for p in range(early, lats):
         mix_lat(p)
 
-    def finish(j, carry):
-        wait(gather_copies(j))
-        return carry
-
-    lax.fori_loop(0, share, finish, 0)
+    drain(all_sem, (), all_out.at[pl.ds(0, genes - 1)] if genes > 1 else None, all_out)
     for p in range(lats):
         wait(mix_back_copies(p))
         mix_keep(p).wait()
 
 
 def lay_body(plan, mix_hbm, all_hbm, mix_out, ind_out, mix_ref, all_ref, row_ref, ind_ref, in_sem, out_sem):
-    subs, lats, depth, _ = mix_hbm.shape
-    parts = [(sub, p) for sub in range(subs) for p in range(lats)]
-    mixes = [
-        pltpu.make_async_copy(mix_hbm.at[sub, p], mix_ref.at[i], in_sem.at[i]) for i, (sub, p) in enumerate(parts)
-    ]
-    outs = [
-        pltpu.make_async_copy(mix_ref.at[i], mix_out.at[pl.ds(i * depth, depth)], out_sem.at[i])
-        for i in range(len(parts))
-    ]
-    whole = pltpu.make_async_copy(all_hbm, all_ref, in_sem.at[len(parts)])
-    for copy in [whole] + mixes:
-        copy.start()
-    whole.wait()
-    last = []
+    codes = pltpu.make_async_copy(all_hbm, all_ref, in_sem.at[0])
+    mix_in = pltpu.make_async_copy(mix_hbm, mix_ref, in_sem.at[1])
+    mix_back = pltpu.make_async_copy(mix_ref, mix_out, out_sem.at[1])
+    codes.start()
+    mix_in.start()
+    codes.wait()
     for owner in range(plan.owners):
         base = owner * plan.share
         for slab in range(plan.split):
@@ -610,39 +603,31 @@
             for r in range(plan.points // 128):
                 first = slab * plan.points + r * 128
                 ind_ref[base : base + plan.share, first : first + 128] = row_ref[gene, :, r, :]
-        if plan.share % 8 == 0:
-            rows = pl.ds(base, plan.share)
-            last.append(pltpu.make_async_copy(ind_ref.at[rows], ind_out.at[rows], out_sem.at[len(parts) + owner]))
-            last[-1].start()
-    if plan.share % 8:
-        last.append(pltpu.make_async_copy(ind_ref, ind_out, out_sem.at[len(parts)]))
-        last[-1].start()
-    for copy, out in zip(mixes, outs):
-        copy.wait()
-        out.start()
-    for copy in outs + last:
-        copy.wait()
+    ind_back = pltpu.make_async_copy(ind_ref, ind_out, out_sem.at[0])
+    ind_back.start()
+    mix_in.wait()
+    mix_back.start()
+    ind_back.wait()
+    mix_back.wait()
 
 
 def lay(plan, mix, codes):
-    subs, lats, depth, genes = mix.shape
-    parts = subs * lats
     anywhere = pl.BlockSpec(memory_space=pl.ANY)
     return pl.pallas_call(
         functools.partial(lay_body, plan),
         in_specs=[anywhere] * 2,
         out_specs=[anywhere] * 2,
         out_shape=[
-            jax.ShapeDtypeStruct((plan.total, genes), F32),
+            jax.ShapeDtypeStruct(mix.shape, F32),
             jax.ShapeDtypeStruct((plan.lats, plan.count), F32),
         ],
         scratch_shapes=[
-            pltpu.VMEM((parts, depth, genes), F32),
+            pltpu.VMEM(mix.shape, F32),
             pltpu.VMEM(codes.shape, jnp.int16),
             pltpu.VMEM((plan.gene, plan.share, plan.points // 128, 128), F32),
             pltpu.VMEM((plan.lats, plan.count), F32),
-            pltpu.SemaphoreType.DMA((parts + 1,)),
-            pltpu.SemaphoreType.DMA((parts + plan.owners,)),
+            pltpu.SemaphoreType.DMA((2,)),
+            pltpu.SemaphoreType.DMA((2,)),
         ],
         compiler_params=pltpu.CompilerParams(vmem_limit_bytes=60 * 2**20),
     )(mix, codes)
@@ -696,15 +681,15 @@
         pltpu.VMEM((plan.points // 128, 128), F32),
         pltpu.VMEM((share, plan.points // 128, 128), jnp.int16),
         pltpu.VMEM((share, blocks, max(1, plan.cached), half, plan.tile), F32),
+        pltpu.VMEM((max(1, far), share, half), sent),
         dma((9,)),
-        dma((2, max(1, flat))),
+        dma((2,)),
         dma((2, 2, max(1, subs - 1))),
-        dma((2, 2, max(1, far))),
-        dma((2, 2, max(1, genes - 1))),
-        dma((2, 2, max(1, flat))),
+        dma((2, 2)),
+        dma((2, 2)),
+        dma((2, 2)),
         dma((2, 3, max(1, subs - 1, lats - 1), lats)),
-        dma((2, share, max(1, genes - 1))),
-        dma((share,)),
+        dma((2,)),
         dma((lats,)),
     ]
     return pl.pallas_call(
@@ -769,7 +754,8 @@
         mixing,
         noise_prec[None, :],
     )
-    return lay(plan, mix, codes)
+    grad_mixing, grad_inducing = lay(plan, mix, codes)
+    return grad_mixing.reshape(mixing.shape), grad_inducing
 
 
 def solution(mesh):

time: 60.8 us -> 60 us (0.987)
  Pallas kernels: 59.9 us -> 59 us
    pallas_call x1, Pallas kernels: 57.4 us -> 56.5 us  [fused(): pl.pallas_call(functools.partial(body, plan), in_specs=[anywhere] * 9, ou...]
where the time goes in v7:
time: 60 us; the launch traced here: 59.8 us
  Pallas kernels  59 us (98%)
  between operations  0.8 us (1%)
    pallas_call x1, Pallas kernels, fused(): pl.pallas_call(functools.partial(body, plan), in_specs=[anywhere] * 9, ou...  56.5 us
    pallas_call x1, Pallas kernels, lay(): pl.pallas_call(functools.partial(lay_body, plan), in_specs=[anywhere] * 2...  2.53 us

profile of v7, /device:TPU:0, one launch (start us, length us, event | category | flops | bytes accessed | tf_op | source)
XLA Modules:
  0.0 59.8 jit_solution(6747623939210186161)
XLA Ops:
  0.6 56.5 %shard_map.104 = (f32[2,2,16,4096]{3,2,1,0:T(8,128)}, s16[4,8,32,128]{3,2,1,0:T(8,128)(2,1)}) custom-call(s32[1,256]{1,0:T(1,128)} %bitcast.6, f32[2,512]{1,0:T(2,128)} %coords_hbm.1, f32[1,32]{1,0:T(1,128)} %bitcast.7, f32[1,32]{1,0:T(1,128)} %bitcast.8, bf16[512,4096]{1,0:T(8,128)(2,1)} %expr_hbm.1, f32[2,32,4096]{2,1,0:T(8,128)} %points_hbm.1, ...), custom_call_target="tpu_custom_call" | custom-call | tf_op jit(solution)/shard_map/pallas_call | solution.py:695
  57.1 2.5 %shard_map.105 = (f32[2,2,16,4096]{3,2,1,0:T(8,128)}, f32[32,4096]{1,0:T(8,128)}) custom-call(f32[2,2,16,4096]{3,2,1,0:T(8,128)} %get-tuple-element.6.mix_hbm, s16[4,8,32,128]{3,2,1,0:T(8,128)(2,1)} %get-tuple-element.7.all_hbm), custom_call_target="tpu_custom_call" | custom-call | tf_op jit(solution)/shard_map/pallas_call | solution.py:616

commit v8 on v7

--- a/solution.py
+++ b/solution.py
@@ -16,7 +16,7 @@
 CENTER = 0.5
 LOG2E = math.log2(math.e)
 PACK = 20
-CACHE = 40 * 2**20
+CACHE = 44 * 2**20
 LEFT = (0, 0, 1, 1, 0, 2)
 RIGHT = (0, 1, 0, 1, 2, 0)
 
@@ -283,13 +283,10 @@
         return lax.rem(me + k, blocks)
 
     def flush(part):
-        lane = lax.broadcasted_iota(jnp.int32, (half, 128), 1)
         for k in range(blocks):
-            sums = jnp.zeros((half, 128), F32)
             for j in range(share):
-                column = jnp.sum(total_ref[j, 2 * k + part], axis=1, keepdims=True)
-                sums = jnp.where(lane == j, column, sums)
-            part_ref[part, lax.rem(ring(k), subs), ring(k) // subs] = sums.T[:share, :]
+                row = jnp.sum(total_ref[j, 2 * k + part].T, axis=0, keepdims=True)
+                part_ref[part, lax.rem(ring(k), subs), ring(k) // subs, j : j + 1, :] = row
         start(near_copies(part))
 
     def forward(units, stages=(), low=0, high=share, step=1):
@@ -485,16 +482,23 @@
             send(all_ref.at[j], all_out.at[g, j], all_sem, (), at(dg=dg)) for dg in range(1, genes)
         ] + [pltpu.make_async_copy(all_ref.at[j], all_out.at[g, j], all_sem.at[1])]
 
-    def backward(part, stages):
-        def step(j, carry):
+    def backward(part, stages, step=1):
+        step = math.gcd(step, share)
+
+        def products(i, carry):
             for when, stage in stages:
-                pl.when(j == when)(stage)
+                pl.when(i == when // step)(stage)
+            for d in range(step):
+                one(i * step + d, d)
+            return carry
+
+        def one(j, slot):
             row = lax.broadcasted_iota(jnp.int32, (plan.turned, 128), 0)
             select = (lax.rem(row, share) == j).astype(F32).astype(BF16)
             for k in range(blocks):
                 place = pl.multiple_of(ring(k) * half, half)
                 turned = lgt_ref[pl.ds(place, half), :]
-                wide_ref[k] = jnp.dot(turned, select, preferred_element_type=F32)
+                wide_ref[slot, k] = jnp.dot(turned, select, preferred_element_type=F32)
             tiles = list(range(plan.points // plan.tile))
             kept = tiles[: plan.cached] if part == 1 else []
             fresh = tiles[len(kept) :]
@@ -516,7 +520,7 @@
 
             def spend(groups):
                 for pack, k, r in groups:
-                    wide = wide_ref[k, r : r + 8, :]
+                    wide = wide_ref[slot, k, r : r + 8, :]
                     for i in pack:
                         t, f = held[i]
                         term = cache_ref[j, k, t, r : r + 8, f * 128 : (f + 1) * 128] * wide
@@ -531,7 +535,7 @@
                         jnp.dot(feat_ref[pl.ds(place, half), :], points, preferred_element_type=F32)
                     )
                     for f in range(lanes):
-                        term = value[:, f * 128 : (f + 1) * 128] * wide_ref[k]
+                        term = value[:, f * 128 : (f + 1) * 128] * wide_ref[slot, k]
                         term = jnp.sum(term.reshape(half // 8, 8, 128), axis=0)
                         sums[f] = term if sums[f] is None else sums[f] + term
                     spend(groups[:pace])
@@ -544,9 +548,8 @@
             if part == 1:
                 all_ref[j] = code(row_ref[...])
                 start(gather_copies(j))
-            return carry
-
-        lax.fori_loop(0, share, step, 0)
+
+        lax.fori_loop(0, share // step, products, 0)
 
     forward([(k, 0) for k in range(1, blocks)], step=2)
     flush(0)
@@ -564,11 +567,12 @@
         0,
         [
             (when(0), lambda: sum_near(1)),
-            (when(3), lambda: middle(1)),
-            (when(3), mix_part),
-            (when(5), lambda: sum_gene(1)),
-            (when(5), mix_sub),
+            (when(4), lambda: middle(1)),
+            (when(4), mix_part),
+            (when(6), lambda: sum_gene(1)),
+            (when(6), mix_sub),
         ],
+        step=2,
     )
     turn(1)
     early = max(1, lats // 2)
@@ -588,12 +592,19 @@
 
 
 def lay_body(plan, mix_hbm, all_hbm, mix_out, ind_out, mix_ref, all_ref, row_ref, ind_ref, in_sem, out_sem):
-    codes = pltpu.make_async_copy(all_hbm, all_ref, in_sem.at[0])
-    mix_in = pltpu.make_async_copy(mix_hbm, mix_ref, in_sem.at[1])
-    mix_back = pltpu.make_async_copy(mix_ref, mix_out, out_sem.at[1])
+    subs, lats = mix_hbm.shape[:2]
+    parts = [(sub, p) for sub in range(subs) for p in range(lats)]
+    codes = pltpu.make_async_copy(all_hbm, all_ref, in_sem.at[len(parts)])
+    mix_in = [
+        pltpu.make_async_copy(mix_hbm.at[part], mix_ref.at[part], in_sem.at[i]) for i, part in enumerate(parts)
+    ]
+    mix_back = [
+        pltpu.make_async_copy(mix_ref.at[part], mix_out.at[part], out_sem.at[i]) for i, part in enumerate(parts)
+    ]
     codes.start()
-    mix_in.start()
     codes.wait()
+    for copy in mix_in:
+        copy.start()
     for owner in range(plan.owners):
         base = owner * plan.share
         for slab in range(plan.split):
@@ -603,12 +614,13 @@
             for r in range(plan.points // 128):
                 first = slab * plan.points + r * 128
                 ind_ref[base : base + plan.share, first : first + 128] = row_ref[gene, :, r, :]
-    ind_back = pltpu.make_async_copy(ind_ref, ind_out, out_sem.at[0])
+    ind_back = pltpu.make_async_copy(ind_ref, ind_out, out_sem.at[len(parts)])
     ind_back.start()
-    mix_in.wait()
-    mix_back.start()
-    ind_back.wait()
-    mix_back.wait()
+    for copy, back in zip(mix_in, mix_back):
+        copy.wait()
+        back.start()
+    for back in mix_back + [ind_back]:
+        back.wait()
 
 
 def lay(plan, mix, codes):
@@ -626,8 +638,8 @@
             pltpu.VMEM(codes.shape, jnp.int16),
             pltpu.VMEM((plan.gene, plan.share, plan.points // 128, 128), F32),
             pltpu.VMEM((plan.lats, plan.count), F32),
-            pltpu.SemaphoreType.DMA((2,)),
-            pltpu.SemaphoreType.DMA((2,)),
+            pltpu.SemaphoreType.DMA((plan.blocks + 1,)),
+            pltpu.SemaphoreType.DMA((plan.blocks + 1,)),
         ],
         compiler_params=pltpu.CompilerParams(vmem_limit_bytes=60 * 2**20),
     )(mix, codes)
@@ -672,7 +684,7 @@
         pltpu.VMEM((2, blocks, share, half), F32),
         pltpu.VMEM((128, half), F32),
         pltpu.VMEM((blocks * half, plan.turned), BF16),
-        pltpu.VMEM((blocks, half, 128), F32),
+        pltpu.VMEM((2, blocks, half, 128), F32),
         pltpu.VMEM((subs, lats, depth, plan.genes), F32),
         pltpu.VMEM((max(1, subs - 1), lats, depth, plan.genes), F32),
         pltpu.VMEM((lats, lats, depth, plan.genes), jnp.int16),

time: 60 us -> 59.7 us (level)
    pallas_call x1, Pallas kernels: 56.5 us -> 55.8 us  [fused(): pl.pallas_call(functools.partial(body, plan), in_specs=[anywhere] * 9, ou...]
where the time goes in v8:
time: 59.7 us; the launch traced here: 59.5 us
  Pallas kernels  58.7 us (98%)
  between operations  0.8 us (1%)
    pallas_call x1, Pallas kernels, fused(): pl.pallas_call(functools.partial(body, plan), in_specs=[anywhere] * 9, ou...  55.8 us
    pallas_call x1, Pallas kernels, lay(): pl.pallas_call(functools.partial(lay_body, plan), in_specs=[anywhere] * 2...  2.95 us

profile of v8, /device:TPU:0, one launch (start us, length us, event | category | flops | bytes accessed | tf_op | source)
XLA Modules:
  0.0 59.5 jit_solution(8247384837465028589)
XLA Ops:
  0.6 55.8 %shard_map.104 = (f32[2,2,16,4096]{3,2,1,0:T(8,128)}, s16[4,8,32,128]{3,2,1,0:T(8,128)(2,1)}) custom-call(s32[1,256]{1,0:T(1,128)} %bitcast.6, f32[2,512]{1,0:T(2,128)} %coords_hbm.1, f32[1,32]{1,0:T(1,128)} %bitcast.7, f32[1,32]{1,0:T(1,128)} %bitcast.8, bf16[512,4096]{1,0:T(8,128)(2,1)} %expr_hbm.1, f32[2,32,4096]{2,1,0:T(8,128)} %points_hbm.1, ...), custom_call_target="tpu_custom_call" | custom-call | tf_op jit(solution)/shard_map/pallas_call | solution.py:707
  56.4 2.9 %shard_map.105 = (f32[2,2,16,4096]{3,2,1,0:T(8,128)}, f32[32,4096]{1,0:T(8,128)}) custom-call(f32[2,2,16,4096]{3,2,1,0:T(8,128)} %get-tuple-element.6.mix_hbm, s16[4,8,32,128]{3,2,1,0:T(8,128)(2,1)} %get-tuple-element.7.all_hbm), custom_call_target="tpu_custom_call" | custom-call | tf_op jit(solution)/shard_map/pallas_call | solution.py:628

commit v9 on v8

--- a/solution.py
+++ b/solution.py
@@ -568,12 +568,12 @@
         [
             (when(0), lambda: sum_near(1)),
             (when(4), lambda: middle(1)),
-            (when(4), mix_part),
+            (when(6), mix_part),
             (when(6), lambda: sum_gene(1)),
-            (when(6), mix_sub),
         ],
         step=2,
     )
+    mix_sub()
     turn(1)
     early = max(1, lats // 2)
 
@@ -601,10 +601,9 @@
     mix_back = [
         pltpu.make_async_copy(mix_ref.at[part], mix_out.at[part], out_sem.at[i]) for i, part in enumerate(parts)
     ]
-    codes.start()
+    for copy in [codes] + mix_in:
+        copy.start()
     codes.wait()
-    for copy in mix_in:
-        copy.start()
     for owner in range(plan.owners):
         base = owner * plan.share
         for slab in range(plan.split):

time: 59.7 us -> 59.3 us (level)
  no operation moved by 1% of the time
where the time goes in v9:
time: 59.3 us; the launch traced here: 59.2 us
  Pallas kernels  58.4 us (98%)
  between operations  0.8 us (1%)
    pallas_call x1, Pallas kernels, fused(): pl.pallas_call(functools.partial(body, plan), in_specs=[anywhere] * 9, ou...  55.8 us
    pallas_call x1, Pallas kernels, lay(): pl.pallas_call(functools.partial(lay_body, plan), in_specs=[anywhere] * 2...  2.57 us

profile of v9, /device:TPU:0, one launch (start us, length us, event | category | flops | bytes accessed | tf_op | source)
XLA Modules:
  0.0 59.2 jit_solution(7638004297625546910)
XLA Ops:
  0.6 55.8 %shard_map.104 = (f32[2,2,16,4096]{3,2,1,0:T(8,128)}, s16[4,8,32,128]{3,2,1,0:T(8,128)(2,1)}) custom-call(s32[1,256]{1,0:T(1,128)} %bitcast.6, f32[2,512]{1,0:T(2,128)} %coords_hbm.1, f32[1,32]{1,0:T(1,128)} %bitcast.7, f32[1,32]{1,0:T(1,128)} %bitcast.8, bf16[512,4096]{1,0:T(8,128)(2,1)} %expr_hbm.1, f32[2,32,4096]{2,1,0:T(8,128)} %points_hbm.1, ...), custom_call_target="tpu_custom_call" | custom-call | tf_op jit(solution)/shard_map/pallas_call | solution.py:706
  56.4 2.6 %shard_map.105 = (f32[2,2,16,4096]{3,2,1,0:T(8,128)}, f32[32,4096]{1,0:T(8,128)}) custom-call(f32[2,2,16,4096]{3,2,1,0:T(8,128)} %get-tuple-element.6.mix_hbm, s16[4,8,32,128]{3,2,1,0:T(8,128)(2,1)} %get-tuple-element.7.all_hbm), custom_call_target="tpu_custom_call" | custom-call | tf_op jit(solution)/shard_map/pallas_call | solution.py:627

commit v10 on v9

--- a/solution.py
+++ b/solution.py
@@ -16,7 +16,7 @@
 CENTER = 0.5
 LOG2E = math.log2(math.e)
 PACK = 20
-CACHE = 44 * 2**20
+CACHE = 40 * 2**20
 LEFT = (0, 0, 1, 1, 0, 2)
 RIGHT = (0, 1, 0, 1, 2, 0)
 
@@ -556,10 +556,12 @@
     forward([(0, 1)], low=when(4), high=when(6), step=2)
     sum_near(0)
     forward([(0, 1)], low=when(6), step=2)
-    forward(
-        [(k, 1) for k in range(1, blocks)],
-        [(when(3), lambda: middle(0)), (when(7), lambda: sum_gene(0))],
-    )
+    others = [(k, 1) for k in range(1, blocks)]
+    forward(others, high=when(3), step=3)
+    middle(0)
+    forward(others, low=when(3), high=when(7), step=4)
+    sum_gene(0)
+    forward(others, low=when(7))
     flush(1)
     lgside_ref[...] = jnp.zeros_like(lgside_ref)
     turn(0)

time: 59.3 us -> 59.7 us (level)
  no operation moved by 1% of the time
where the time goes in v10:
time: 59.7 us; the launch traced here: 59.6 us
  Pallas kernels  58.7 us (98%)
  between operations  0.82 us (1%)
    pallas_call x1, Pallas kernels, fused(): pl.pallas_call(functools.partial(body, plan), in_specs=[anywhere] * 9, ou...  56.2 us
    pallas_call x1, Pallas kernels, lay(): pl.pallas_call(functools.partial(lay_body, plan), in_specs=[anywhere] * 2...  2.57 us

profile of v10, /device:TPU:0, one launch (start us, length us, event | category | flops | bytes accessed | tf_op | source)
XLA Modules:
  0.0 59.6 jit_solution(17621016809756863271)
XLA Ops:
  0.6 56.2 %shard_map.104 = (f32[2,2,16,4096]{3,2,1,0:T(8,128)}, s16[4,8,32,128]{3,2,1,0:T(8,128)(2,1)}) custom-call(s32[1,256]{1,0:T(1,128)} %bitcast.6, f32[2,512]{1,0:T(2,128)} %coords_hbm.1, f32[1,32]{1,0:T(1,128)} %bitcast.7, f32[1,32]{1,0:T(1,128)} %bitcast.8, bf16[512,4096]{1,0:T(8,128)(2,1)} %expr_hbm.1, f32[2,32,4096]{2,1,0:T(8,128)} %points_hbm.1, ...), custom_call_target="tpu_custom_call" | custom-call | tf_op jit(solution)/shard_map/pallas_call | solution.py:708
  56.8 2.6 %shard_map.105 = (f32[2,2,16,4096]{3,2,1,0:T(8,128)}, f32[32,4096]{1,0:T(8,128)}) custom-call(f32[2,2,16,4096]{3,2,1,0:T(8,128)} %get-tuple-element.6.mix_hbm, s16[4,8,32,128]{3,2,1,0:T(8,128)(2,1)} %get-tuple-element.7.all_hbm), custom_call_target="tpu_custom_call" | custom-call | tf_op jit(solution)/shard_map/pallas_call | solution.py:629
